TPU v7x, 256 devices: a whole 4x4x8 slice. The times are simulated.
256 devices in a mesh: wide: 16 (over y, x), narrow: 16 (over z, core).
Axes of the slice: x: 4, y: 4, z: 8, core: 2. Of those that a mesh axis runs over, the one named last changes fastest.
Arguments:
- anomalies: bfloat16 [256, 262144], P(None, ('wide', 'narrow')), may hold values from -16 to 16
- sketch: bfloat16 [128, 256], replicated, may hold values from -0.375 to 0.375
Outputs:
- eofs: float32 [128, 262144], P(None, ('wide', 'narrow'))
- pcs: float32 [128, 256], replicated
All inputs are finite; a program needn't handle non-finite values.
Results may differ from a plain program's by a relative error of at most 0.0044.
Values may be sent and summed in bfloat16 or wider, within the bound.
No kernel may reach another device: no remote copies, remote signals or barrier semaphores. Data moves between devices by JAX's collectives and lax.ppermute only.
A program may use at most 64 MiB of HBM per device.

v0:
```python
import jax
import jax.numpy as jnp
from jax import lax
from jax.sharding import Mesh
from jax.sharding import PartitionSpec as P

NARROW = ("narrow_0", "narrow_1")
WIDE = ("wide_0", "wide_1")
WIDE_NARROW = ("wide_0", "wide_1", "narrow_0", "narrow_1")


def over_pieces(array, axis):
    pieces = lax.all_gather(array, axis)
    return pieces.sum(axis=0)


def sent_to_all(array, axis):
    copies = jnp.broadcast_to(array, (lax.axis_size(axis), *array.shape))
    return lax.all_to_all(copies, axis, split_axis=0, concat_axis=0, tiled=True)


def taken_together(array, axis):
    everything = sent_to_all(array, axis)
    return jnp.sum(everything, axis=0)


def cut_along(array, dim, count):
    before, after = (array.shape[:dim], array.shape[dim + 1 :])
    return jnp.moveaxis(array.reshape(*before, count, -1, *after), dim, 0)


def sent_and_summed(array, axis, dim):
    count = lax.axis_size(axis)
    pieces = lax.all_to_all(cut_along(array, dim, count), axis, 0, 0, tiled=True)
    return jnp.sum(pieces, axis=0)


def sum_by_axis(array, axes, dim):
    far, near = axes
    pieces = cut_along(array, dim, lax.axis_size(far))
    nearer = sent_and_summed(pieces, near, dim + 1)
    arrived = lax.all_to_all(nearer, far, split_axis=0, concat_axis=0, tiled=True)
    return arrived.sum(axis=0)


def rows_for(lines, count):
    spare = -len(lines) % count
    return jnp.pad(lines, [(0, spare)] + [(0, 0)] * (lines.ndim - 1))


def laid_out(pieces, dim):
    pieces = jnp.moveaxis(pieces, 0, dim)
    lengths = pieces.shape
    return pieces.reshape(*lengths[:dim], lengths[dim] * lengths[dim + 1], *lengths[dim + 2 :])


def gather_axes(array, axes, dim):
    far, near = axes
    pieces = sent_to_all(sent_to_all(array, far), near)
    return laid_out(pieces.swapaxes(0, 1).reshape(-1, *array.shape), dim)


def sum_by_parts(array, axes):
    lines = array.reshape(-1)
    own = sum_by_axis(rows_for(lines, lax.axis_size(axes[0]) * lax.axis_size(axes[1])), axes, 0)
    whole = gather_axes(own, axes, 0)
    return whole[: len(lines)].reshape(array.shape)


def gram_total(matrix):
    local_gram = jnp.dot(
        matrix, matrix.T, precision=lax.Precision.HIGHEST, preferred_element_type=jnp.float32
    )
    inner_sum = over_pieces(local_gram, NARROW)
    return taken_together(inner_sum, WIDE)


def lower_solve(lower_factor, matrix):
    return lax.linalg.triangular_solve(lower_factor, matrix, left_side=True, lower=True)


def orthonormal(matrix):
    lower_factor = jnp.linalg.cholesky(gram_total(matrix))
    middle = lower_solve(lower_factor, matrix)
    second_lower = jnp.linalg.cholesky(gram_total(middle))
    return lower_solve(second_lower, middle)


def project_days(rows, anomalies):
    return lax.dot_general(
        rows, anomalies, (((1,), (1,)), ((), ())), preferred_element_type=jnp.float32
    )


def local(anomalies, sketch):
    first = jnp.dot(sketch, anomalies, preferred_element_type=jnp.float32)
    basis = orthonormal(first).astype(jnp.bfloat16)
    partial_days = project_days(basis, anomalies)
    back = sum_by_parts(partial_days, ("wide_0", ("wide_1", "narrow_0", "narrow_1"))).astype(
        jnp.bfloat16
    )
    second = jnp.dot(back, anomalies, preferred_element_type=jnp.float32)
    refined = orthonormal(second)
    total_cells = anomalies.shape[1] * lax.axis_size(WIDE) * lax.axis_size(NARROW)
    day_scale = jnp.sqrt(jnp.float32(anomalies.shape[0]) / jnp.float32(total_cells))
    projected = project_days(refined.astype(jnp.bfloat16), anomalies)
    pcs = sum_by_parts(projected, ("wide_0", ("wide_1", "narrow_0", "narrow_1"))) * day_scale
    eofs = refined * jnp.sqrt(jnp.float32(total_cells))
    return (eofs, pcs)


def solution(mesh):
    split = Mesh(mesh.devices.reshape(4, 4, 8, 2), ("wide_0", "wide_1", "narrow_0", "narrow_1"))
    in_specs = (P(None, WIDE_NARROW), P())
    out_specs = (P(None, WIDE_NARROW), P())
    return jax.shard_map(local, mesh=split, in_specs=in_specs, out_specs=out_specs, check_vma=False)
```

profile of v0, /device:TPU:1, one launch (start us, length us, event | category | flops | bytes accessed | tf_op | source)
XLA Modules:
  0.0 454.8 jit_solution(3265269187996252585)
XLA Ops:
  7.2 1.0 copy-done
  8.2 1.1 fusion.23
  9.3 1.2 fusion.24
  10.6 42.8 %all-gather.9.cloned.1.call-done = f32[2048,128]{1,0:T(8,128)} async-done(((f32[128,128]{1,0:T(8,128)}), f32[2048,128]{1,0:T(8,128)}) %all-gather.9.cloned.1.call-update) | async-done | bytes 1048592 | tf_op jit(solution)/shard_map/all_gather | solution.py:13
  53.4 1.3 reduce_sum.108
  54.8 22.8 %all_to_all.76 = f32[16,128,128]{2,1,0:T(8,128)S(1)} all-to-all(f32[16,128,128]{2,1,0:T(8,128)S(1)} %broadcast_in_dim.25), channel_id=1, replica_groups=mesh['wide_0'=4,'wide_1'=4,'narrow_0'=8,'narrow_1'=2] {'wide_0','wide_1'}, dimensions={0} | all-to-all | bytes 2097152 | tf_op jit(solution)/shard_map/all_to_all | solution.py:19
  77.7 11.7 %cholesky.74 = f32[128,128]{1,0:T(8,128)S(1)} custom-call(f32[128,128]{1,0:T(8,128)S(1)} %fusion.16), custom_call_target="Cholesky" | custom-call | tf_op jit(solution)/shard_map/jit(cholesky)/cholesky | solution.py:83
  89.5 0.6 compare_reduce_fusion.3
  90.1 0.7 fusion.2
  90.8 9.8 %custom-call.8 = f32[1,128,128]{1,2,0:T(8,128)S(1)} custom-call(f32[1,128,128]{2,1,0:T(8,128)S(1)} %fusion.2), custom_call_target="InvertDiagBlocksLowerTriangular" | custom-call | tf_op jit(solution)/shard_map/triangular_solve/custom-call.0 | solution.py:79
  100.6 0.6 fusion.14
  101.2 1.2 fusion.25
  102.5 34.9 %all-gather.11.cloned.1.call-done = f32[2048,128]{1,0:T(8,128)} async-done(((f32[128,128]{1,0:T(8,128)}), f32[2048,128]{1,0:T(8,128)}) %all-gather.11.cloned.1.call-update) | async-done | bytes 1048592 | tf_op jit(solution)/shard_map/all_gather | solution.py:13
  137.4 1.3 reduce_sum.110
  138.8 23.2 %all_to_all.77 = f32[16,128,128]{2,1,0:T(8,128)S(1)} all-to-all(f32[16,128,128]{2,1,0:T(8,128)S(1)} %broadcast_in_dim.26), channel_id=1, replica_groups=mesh['wide_0'=4,'wide_1'=4,'narrow_0'=8,'narrow_1'=2] {'wide_0','wide_1'}, dimensions={0} | all-to-all | bytes 2097152 | tf_op jit(solution)/shard_map/all_to_all | solution.py:19
  162.2 11.7 %cholesky.85 = f32[128,128]{1,0:T(8,128)S(1)} custom-call(f32[128,128]{1,0:T(8,128)S(1)} %fusion.13), custom_call_target="Cholesky" | custom-call | tf_op jit(solution)/shard_map/jit(cholesky)/cholesky | solution.py:85
  173.9 0.6 compare_reduce_fusion.2
  174.6 0.7 fusion.3
  175.2 9.8 %custom-call.9 = f32[1,128,128]{1,2,0:T(8,128)S(1)} custom-call(f32[1,128,128]{2,1,0:T(8,128)S(1)} %fusion.3), custom_call_target="InvertDiagBlocksLowerTriangular" | custom-call | tf_op jit(solution)/shard_map/triangular_solve/custom-call.0 | solution.py:79
  185.0 0.6 convolution_convert_fusion
  185.7 0.3 fusion.26
  186.1 16.9 %all_to_all.78 = f32[64,4,128]{2,1,0:T(4,128)S(1)} all-to-all(f32[64,4,128]{2,1,0:T(4,128)S(1)} %bitcast.81), channel_id=1, replica_groups=mesh['wide_0'=4,'wide_1'=4,'narrow_0'=8,'narrow_1'=2] {'wide_1','narrow_..., dimensions={0} | all-to-all | bytes 262144 | tf_op jit(solution)/shard_map/all_to_all | solution.py:34
  203.1 6.5 %all_to_all.79 = f32[4,1,128]{2,1,0:T(1,128)S(1)} all-to-all(f32[4,1,128]{2,1,0:T(1,128)S(1)} %bitcast.84), channel_id=1, replica_groups=mesh['wide_0'=4,'wide_1'=4,'narrow_0'=8,'narrow_1'=2] {'wide_0'}, dimensions={0} | all-to-all | bytes 4096 | tf_op jit(solution)/shard_map/all_to_all | solution.py:42
  209.5 6.5 %all_to_all.80 = f32[4,1,128]{2,1,0:T(1,128)S(1)} all-to-all(f32[4,1,128]{2,1,0:T(1,128)S(1)} %broadcast_in_dim.27), channel_id=1, replica_groups=mesh['wide_0'=4,'wide_1'=4,'narrow_0'=8,'narrow_1'=2] {'wide_0'}, dimensions={0} | all-to-all | bytes 4096 | tf_op jit(solution)/shard_map/all_to_all | solution.py:19
  216.0 16.9 %all_to_all.81 = bf16[64,4,128]{2,1,0:T(4,128)(2,1)S(1)} all-to-all(bf16[64,4,128]{2,1,0:T(4,128)(2,1)S(1)} %broadcast_in_dim.28), channel_id=1, replica_groups=mesh['wide_0'=4,'wide_1'=4,'narrow_0'=8,'narrow_1'=2] {'wide_1','narrow_..., dimensions={0} | all-to-all | bytes 131072 | tf_op jit(solution)/shard_map/all_to_all | solution.py:19
  233.2 1.2 fusion.28
  234.5 31.9 %all-gather.13.cloned.1.call-done = f32[2048,128]{1,0:T(8,128)} async-done(((f32[128,128]{1,0:T(8,128)}), f32[2048,128]{1,0:T(8,128)}) %all-gather.13.cloned.1.call-update) | async-done | bytes 1048592 | tf_op jit(solution)/shard_map/all_gather | solution.py:13
  266.4 1.3 reduce_sum.114
  267.8 22.9 %all_to_all.82 = f32[16,128,128]{2,1,0:T(8,128)S(1)} all-to-all(f32[16,128,128]{2,1,0:T(8,128)S(1)} %broadcast_in_dim.29), channel_id=1, replica_groups=mesh['wide_0'=4,'wide_1'=4,'narrow_0'=8,'narrow_1'=2] {'wide_0','wide_1'}, dimensions={0} | all-to-all | bytes 2097152 | tf_op jit(solution)/shard_map/all_to_all | solution.py:19
  290.9 11.7 %cholesky.96 = f32[128,128]{1,0:T(8,128)S(1)} custom-call(f32[128,128]{1,0:T(8,128)S(1)} %fusion.11), custom_call_target="Cholesky" | custom-call | tf_op jit(solution)/shard_map/jit(cholesky)/cholesky | solution.py:83
  302.7 0.6 compare_reduce_fusion.1
  303.3 0.7 fusion.4
  304.0 9.8 %custom-call.10 = f32[1,128,128]{1,2,0:T(8,128)S(1)} custom-call(f32[1,128,128]{2,1,0:T(8,128)S(1)} %fusion.4), custom_call_target="InvertDiagBlocksLowerTriangular" | custom-call | tf_op jit(solution)/shard_map/triangular_solve/custom-call.0 | solution.py:79
  313.8 0.6 fusion.9
  314.4 1.2 fusion.29
  315.7 34.9 %all-gather.15.cloned.1.call-done = f32[2048,128]{1,0:T(8,128)} async-done(((f32[128,128]{1,0:T(8,128)}), f32[2048,128]{1,0:T(8,128)}) %all-gather.15.cloned.1.call-update) | async-done | bytes 1048592 | tf_op jit(solution)/shard_map/all_gather | solution.py:13
  350.6 1.3 reduce_sum.116
  352.0 23.0 %all_to_all.83 = f32[16,128,128]{2,1,0:T(8,128)S(1)} all-to-all(f32[16,128,128]{2,1,0:T(8,128)S(1)} %broadcast_in_dim.30), channel_id=1, replica_groups=mesh['wide_0'=4,'wide_1'=4,'narrow_0'=8,'narrow_1'=2] {'wide_0','wide_1'}, dimensions={0} | all-to-all | bytes 2097152 | tf_op jit(solution)/shard_map/all_to_all | solution.py:19
  375.1 11.7 %cholesky.107 = f32[128,128]{1,0:T(8,128)S(1)} custom-call(f32[128,128]{1,0:T(8,128)S(1)} %fusion.8), custom_call_target="Cholesky" | custom-call | tf_op jit(solution)/shard_map/jit(cholesky)/cholesky | solution.py:85
  386.9 0.6 compare_reduce_fusion
  387.5 0.7 fusion.5
  388.2 9.8 %custom-call.11 = f32[1,128,128]{1,2,0:T(8,128)S(1)} custom-call(f32[1,128,128]{2,1,0:T(8,128)S(1)} %fusion.5), custom_call_target="InvertDiagBlocksLowerTriangular" | custom-call | tf_op jit(solution)/shard_map/triangular_solve/custom-call.0 | solution.py:79
  398.0 1.4 broadcast_multiply_fusion
  399.9 16.9 %all_to_all.84 = f32[64,4,128]{2,1,0:T(4,128)S(1)} all-to-all(f32[64,4,128]{2,1,0:T(4,128)S(1)} %bitcast.82), channel_id=1, replica_groups=mesh['wide_0'=4,'wide_1'=4,'narrow_0'=8,'narrow_1'=2] {'wide_1','narrow_..., dimensions={0} | all-to-all | bytes 262144 | tf_op jit(solution)/shard_map/all_to_all | solution.py:34
  416.8 6.5 %all_to_all.85 = f32[4,1,128]{2,1,0:T(1,128)S(1)} all-to-all(f32[4,1,128]{2,1,0:T(1,128)S(1)} %bitcast.85), channel_id=1, replica_groups=mesh['wide_0'=4,'wide_1'=4,'narrow_0'=8,'narrow_1'=2] {'wide_0'}, dimensions={0} | all-to-all | bytes 4096 | tf_op jit(solution)/shard_map/all_to_all | solution.py:42
  423.3 6.5 %all_to_all.86 = f32[4,1,128]{2,1,0:T(1,128)S(1)} all-to-all(f32[4,1,128]{2,1,0:T(1,128)S(1)} %broadcast_in_dim.31), channel_id=1, replica_groups=mesh['wide_0'=4,'wide_1'=4,'narrow_0'=8,'narrow_1'=2] {'wide_0'}, dimensions={0} | all-to-all | bytes 4096 | tf_op jit(solution)/shard_map/all_to_all | solution.py:19
  429.8 17.5 %all_to_all.87 = f32[64,4,128]{2,1,0:T(4,128)S(1)} all-to-all(f32[64,4,128]{2,1,0:T(4,128)S(1)} %broadcast_in_dim.32), channel_id=1, replica_groups=mesh['wide_0'=4,'wide_1'=4,'narrow_0'=8,'narrow_1'=2] {'wide_1','narrow_..., dimensions={0} | all-to-all | bytes 262144 | tf_op jit(solution)/shard_map/all_to_all | solution.py:19
  447.3 0.7 mul.23
  (47 shorter events, 2.5 us)
Async XLA Ops:
  7.2 1.0 copy-start
  7.2 46.2 %all-gather.9.cloned.1.call-start = ((), (), s32[]{:S(2)}) async-start(), calls=%async_computation.12 | async-start | bytes 1114112 | tf_op jit(solution)/shard_map/all_gather | solution.py:13
  10.5 126.9 %all-gather.11.cloned.1.call-start = ((), (), s32[]{:S(2)}) async-start(), calls=%async_computation.13 | async-start | bytes 1114112 | tf_op jit(solution)/shard_map/all_gather | solution.py:13
  102.5 164.0 %all-gather.13.cloned.1.call-start = ((), (), s32[]{:S(2)}) async-start(), calls=%async_computation.14 | async-start | bytes 1114112 | tf_op jit(solution)/shard_map/all_gather | solution.py:13
  234.5 116.1 %all-gather.15.cloned.1.call-start = ((), (), s32[]{:S(2)}) async-start(), calls=%async_computation.15 | async-start | bytes 1114112 | tf_op jit(solution)/shard_map/all_gather | solution.py:13
Sparse Core Ops, SparseCore 0:
  10.6 42.7 all-gather.8
  102.6 34.7 all-gather.10
  234.6 31.7 all-gather.12
  315.8 34.7 all-gather.14
where the time goes:
time: 462 us; the launch traced here: 455 us
  blocking collectives  186 us (40%)
  waiting for transfers between devices  145 us (31%)
  other arithmetic  97.1 us (21%)
  between operations  14.3 us (3%)
  matrix products  10.1 us (2%)
    all_gather x4, waiting for transfers between devices, over_pieces(): pieces = lax.all_gather(array, axis)  145 us
    all_to_all x8, blocking collectives, sent_to_all(): return lax.all_to_all(copies, axis, split_axis=0, concat_axis=0, tiled=True)  139 us
    another operation x8, other arithmetic, lower_solve(): lax.linalg.triangular_solve(lower_factor, matrix, left_side=True, lower=T...  41.9 us
    all_to_all x2, blocking collectives, sent_and_summed(): lax.all_to_all(cut_along(array, dim, count), axis, 0, 0, tiled=True)  33.7 us
    another operation x6, other arithmetic, orthonormal(): lower_factor = jnp.linalg.cholesky(gram_total(matrix))  24.8 us
    another operation x6, other arithmetic, orthonormal(): second_lower = jnp.linalg.cholesky(gram_total(middle))  24.8 us
    all_to_all x2, blocking collectives, sum_by_axis(): lax.all_to_all(nearer, far, split_axis=0, concat_axis=0, tiled=True)  12.9 us
  transfers between devices with their start and end apart: 4, of which 4 were waited for; matrix products, arithmetic and copies ran while one was open for 0% of the time, Pallas kernels for 0%

commit v1 on v0

v1 whole, which is shorter than its diff:
```python
import functools

import jax
import jax.numpy as jnp
from jax import lax
from jax.experimental import pallas as pl
from jax.experimental.pallas import tpu as pltpu
from jax.sharding import Mesh
from jax.sharding import PartitionSpec as P

PLANE = ("y", "x")
CELL_AXES = ("y", "x", "z", "core")
RANK = 128
DAYS = 256
SUB = 8
PANEL = 4
NEAR = 1e-4
HIGHEST = lax.Precision.HIGHEST


def dot(a, b, dims=((1,), (0,))):
    return lax.dot_general(
        a, b, (dims, ((), ())), precision=HIGHEST, preferred_element_type=jnp.float32
    )


def dot_nt(a, b):
    return dot(a, b, ((1,), (1,)))


def pieces(a):
    high = a.astype(jnp.bfloat16)
    rest = a - high.astype(jnp.float32)
    middle = rest.astype(jnp.bfloat16)
    low = (rest - middle.astype(jnp.float32)).astype(jnp.bfloat16)
    return high, middle, low


def dot_right(a, split, dims=((1,), (0,))):
    high, middle, low = (
        lax.dot_general(a, b, (dims, ((), ())), preferred_element_type=jnp.float32) for b in split
    )
    return high + (middle + low)


def dot_left(split, b, dims=((1,), (0,))):
    high, middle, low = (
        lax.dot_general(a, b, (dims, ((), ())), preferred_element_type=jnp.float32) for a in split
    )
    return high + (middle + low)


def spread(a):
    return jnp.broadcast_to(a, (SUB, RANK))


def eliminated(gram):
    lane = lax.broadcasted_iota(jnp.int32, (SUB, RANK), 1)
    sub = lax.broadcasted_iota(jnp.int32, (SUB, RANK), 0)
    rows = [gram[SUB * b : SUB * (b + 1), :] for b in range(RANK // SUB)]
    scales = []
    for b in range(RANK // SUB):
        scale = jnp.ones((SUB, RANK), jnp.float32)
        for k in range(0, SUB, PANEL):
            j = SUB * b + k
            top = [spread(rows[b][k + t : k + t + 1, :]) for t in range(PANEL)]
            s = {
                (t, u): spread(top[t][:, j + u : j + u + 1])
                for t in range(PANEL)
                for u in range(t, PANEL)
            }
            factor, ratio = [], {}
            for t in range(PANEL):
                inverse = 1.0 / s[t, t]
                scale = jnp.where(sub == k + t, s[t, t], scale)
                factor.append(jnp.where(lane == j + t, 1.0, top[t]) * inverse)
                for u in range(t + 1, PANEL):
                    ratio[t, u] = s[t, u] * inverse
                for u in range(t + 1, PANEL):
                    top[u] = jnp.where(lane == j + t, 0.0, top[u]) - s[t, u] * factor[t]
                    for v in range(u, PANEL):
                        s[u, v] = s[u, v] - ratio[t, u] * s[t, v]
            in_panel = (lane >= j) & (lane < j + PANEL)
            update = [
                jnp.where((lane > j + t) & (lane < j + PANEL), 0.0, factor[t])
                for t in range(PANEL)
            ]
            for i in range(b if k + PANEL < SUB else b + 1, RANK // SUB):
                column = [spread(rows[i][:, j + t : j + t + 1]) for t in range(PANEL)]
                for t in range(PANEL):
                    for u in range(t + 1, PANEL):
                        column[u] = column[u] - column[t] * ratio[t, u]
                total = column[0] * update[0]
                for t in range(1, PANEL):
                    total = total + column[t] * update[t]
                changed = jnp.where(in_panel, 0.0, rows[i]) - total
                if i == b:
                    changed = jnp.where(sub >= k + PANEL, changed, rows[i])
                rows[i] = changed
            for t in range(PANEL):
                rows[b] = jnp.where(sub == k + t, top[t], rows[b])
        scales.append(scale)
    out = []
    for b in range(RANK // SUB):
        place = lane - (sub + SUB * b)
        unit = jnp.where(place < 0, rows[b], jnp.where(place == 0, 1.0, 0.0))
        out.append(unit * lax.rsqrt(scales[b]))
    return jnp.concatenate(out, axis=0)


def half_lower(a, row, column):
    return jnp.where(row > column, a, jnp.where(row == column, 0.5 * a, 0.0))


def whitened(gram, out_ref):
    row = lax.broadcasted_iota(jnp.int32, (RANK, RANK), 0)
    column = lax.broadcasted_iota(jnp.int32, (RANK, RANK), 1)
    identity = jnp.where(row == column, 1.0, 0.0)
    error = gram - identity
    near = jnp.sum(error * error) < NEAR

    @pl.when(near)
    def _():
        first = identity - half_lower(error, row, column)
        left = dot_nt(dot(first, gram), first) - identity
        out_ref[...] = first - dot(half_lower(left, row, column), first)

    @pl.when(jnp.logical_not(near))
    def _():
        out_ref[...] = eliminated(gram)


def algebra(cells, mine_ref, other_ref, core_ref, sketch_ref, anomalies_ref, eofs_ref, pcs_ref, inv_ref):
    first_core = core_ref[0, 0] == 0
    mine, other = mine_ref[...], other_ref[...]
    covariance = jnp.concatenate(
        [jnp.where(first_core, mine, other), jnp.where(first_core, other, mine)], axis=1
    )
    parts = pieces(covariance)
    sketch = sketch_ref[...]
    seen = dot_right(sketch, parts)
    gram = dot_left(pieces(seen), sketch, ((1,), (1,)))
    inverse = eliminated(gram)
    rows = dot_left(pieces(inverse), sketch)
    whitened(dot_nt(dot(rows, covariance), rows), inv_ref)
    back = dot(inv_ref[...], dot(inverse, seen)).astype(jnp.bfloat16)
    gram = dot_left(pieces(dot_right(back, parts)), back, ((1,), (1,)))
    inverse = eliminated(gram)
    rows = dot_left(pieces(inverse), back)
    days = dot(rows, covariance)
    whitened(dot_nt(days, rows), inv_ref)
    inverse = inv_ref[...]
    pcs_ref[...] = dot(inverse, days) * jnp.sqrt(jnp.float32(DAYS) / jnp.float32(cells))
    refined = dot(inverse, rows)
    eofs_ref[...] = dot_left(pieces(refined), anomalies_ref[...]) * jnp.sqrt(jnp.float32(cells))


def exchanged(array):
    return lax.ppermute(array, "core", [(0, 1), (1, 0)])


def all_to_all(array, axes):
    return lax.all_to_all(array, axes, split_axis=0, concat_axis=0, tiled=True)


def sent_to_all(array, axes):
    return all_to_all(jnp.broadcast_to(array, (lax.axis_size(axes), *array.shape)), axes)


def summed_halves(anomalies):
    core = lax.axis_index("core")
    product = lax.dot_general(
        anomalies, anomalies, (((1,), (1,)), ((), ())), preferred_element_type=jnp.float32
    )
    halves = jnp.stack([product[:, :RANK], product[:, RANK:]])
    own = lax.dynamic_index_in_dim(halves, core, 0, False)
    partner = lax.dynamic_index_in_dim(halves, 1 - core, 0, False)
    half = own + exchanged(partner)
    count = lax.axis_size(PLANE)
    share = all_to_all(half.reshape(count, -1, RANK), PLANE).sum(axis=0)
    share = sent_to_all(share, "z").sum(axis=0)
    return sent_to_all(share, PLANE).reshape(DAYS, RANK)


def local(anomalies, sketch):
    mine = summed_halves(anomalies)
    other = exchanged(mine)
    core = lax.axis_index("core").astype(jnp.int32).reshape(1, 1)
    cells = anomalies.shape[1] * lax.axis_size(CELL_AXES)
    vmem = pl.BlockSpec(memory_space=pltpu.VMEM)
    smem = pl.BlockSpec(memory_space=pltpu.SMEM)
    return pl.pallas_call(
        functools.partial(algebra, cells),
        out_shape=(
            jax.ShapeDtypeStruct((RANK, anomalies.shape[1]), jnp.float32),
            jax.ShapeDtypeStruct((RANK, DAYS), jnp.float32),
        ),
        in_specs=[vmem, vmem, smem, vmem, vmem],
        out_specs=(vmem, vmem),
        scratch_shapes=[pltpu.VMEM((RANK, RANK), jnp.float32)],
        name="algebra",
    )(mine, other, core, sketch, anomalies)


def solution(mesh):
    split = Mesh(mesh.devices.reshape(4, 4, 8, 2), CELL_AXES)
    in_specs = (P(None, CELL_AXES), P())
    out_specs = (P(None, CELL_AXES), P())
    return jax.shard_map(local, mesh=split, in_specs=in_specs, out_specs=out_specs, check_vma=False)
```

time: 462 us -> 69.1 us (0.15); the launches traced: 455 us -> 68.9 us
  blocking collectives: 186 us -> 36.9 us
  waiting for transfers between devices: 145 us -> 1.97 us
  other arithmetic: 97.1 us -> 0.1 us
  Pallas kernels: 0 us -> 19.3 us
  between operations: 14.3 us -> 0.69 us
  matrix products: 10.1 us -> 1.66 us
  starting transfers between devices: 0.16 us -> 7.54 us
    all_to_all x12 -> x3, blocking collectives: 186 us -> 36.9 us  [all_to_all(): return lax.all_to_all(array, axes, split_axis=0, concat_axis=0, tiled=True)]
    all_gather x4 -> x0, waiting for transfers between devices: 145 us -> none  [over_pieces(): pieces = lax.all_gather(array, axis)]
    another operation x20 -> x0, other arithmetic: 91.4 us -> none  [the longest x8 41.9 us: lower_solve(): lax.linalg.triangular_solve(lower_factor, matrix, left_side=True, lower=T...]
    pallas_call x0 -> x1, Pallas kernels: none -> 19.3 us  [local(): pl.pallas_call(functools.partial(algebra, cells), out_shape=(jax.ShapeDty...]
    ppermute x0 -> x2, starting transfers between devices: none -> 7.54 us  [exchanged(): return lax.ppermute(array, 'core', [(0, 1), (1, 0)])]
    reduce_sum x12 -> x2, other arithmetic: 5.57 us -> 0.03 us  [the longest x1 0.02 us: summed_halves(): share = all_to_all(half.reshape(count, -1, RANK), PLANE).sum(axis=0)]
    dot_general x8 -> x1, matrix products: 6.77 us -> 1.66 us  [summed_halves(): lax.dot_general(anomalies, anomalies, (((1,), (1,)), ((), ())), preferred...]
  transfers between devices with their start and end apart: 4 -> 2, of which waited for: 4 -> 2; matrix products, arithmetic and copies ran while one was open for 0% -> 0% of each run, Pallas kernels for 0% -> 0%
where the time goes in v1:
time: 69.1 us; the launch traced here: 68.9 us
  blocking collectives  36.9 us (53%)
  Pallas kernels  19.3 us (28%)
  starting transfers between devices  7.54 us (11%)
  waiting for transfers between devices  1.97 us (3%)
  matrix products  1.66 us (2%)
    all_to_all x3, blocking collectives, all_to_all(): return lax.all_to_all(array, axes, split_axis=0, concat_axis=0, tiled=True)  36.9 us
    pallas_call x1, Pallas kernels, local(): pl.pallas_call(functools.partial(algebra, cells), out_shape=(jax.ShapeDty...  19.3 us
    ppermute x2, starting transfers between devices, exchanged(): return lax.ppermute(array, 'core', [(0, 1), (1, 0)])  7.54 us
    ppermute x2, waiting for transfers between devices, exchanged(): return lax.ppermute(array, 'core', [(0, 1), (1, 0)])  1.97 us
    dot_general x1, matrix products, summed_halves(): lax.dot_general(anomalies, anomalies, (((1,), (1,)), ((), ())), preferred...  1.66 us
  transfers between devices with their start and end apart: 2, of which 2 were waited for; matrix products, arithmetic and copies ran while one was open for 0% of the time, Pallas kernels for 0%

profile of v1, /device:TPU:1, one launch (start us, length us, event | category | flops | bytes accessed | tf_op | source)
XLA Modules:
  0.0 68.9 jit_solution(4574472123251434540)
XLA Ops:
  0.6 1.7 %fusion.5 = f32[256,256]{1,0:T(8,128)S(1)} fusion(bf16[256,1024]{1,0:T(8,128)(2,1)} %anomalies_ref.1), kind=kOutput, calls=%fused_computation.11 | convolution fusion | flops 134217728 | bytes 786432 | tf_op jit(solution)/shard_map/dot_general | solution.py:172
  2.4 3.3 %collective-permute-start = (f32[256,128]{1,0:T(8,128)S(1)}, f32[256,128]{1,0:T(8,128)S(1)}, u32[]{:S(2)}, u32[]{:S(2)}) collective-permute-start(f32[256,128]{1,0:T(8,128)S(1)} %fusion.1), channel_id=1, source_target_pairs={{0,1},{1,0},{2,3},{3,2},{4,5},{5,4},{6,7},{7,6},{8,9},{9,8},{10,11... | collective-permute-start | bytes 393224 | tf_op jit(solution)/shard_map/ppermute | solution.py:159
  5.7 1.0 %collective-permute-done = f32[256,128]{1,0:T(8,128)S(1)} collective-permute-done((f32[256,128]{1,0:T(8,128)S(1)}, f32[256,128]{1,0:T(8,128)S(1)}, u32[]{:S(2)}, u32[]{:S(2)}) %collective-permute-start) | collective-permute-done | bytes 131104 | tf_op jit(solution)/shard_map/ppermute | solution.py:159
  6.7 11.7 %all_to_all.15 = f32[16,16,128]{2,1,0:T(8,128)S(1)} all-to-all(f32[16,16,128]{2,1,0:T(8,128)S(1)} %bitcast.15), channel_id=1, replica_groups=mesh['y'=4,'x'=4,'z'=8,'core'=2] {'y','x'}, dimensions={0} | all-to-all | bytes 262144 | tf_op jit(solution)/shard_map/all_to_all | solution.py:163
  18.4 15.2 %all_to_all.16 = f32[8,16,128]{2,1,0:T(8,128)S(1)} all-to-all(f32[8,16,128]{2,1,0:T(8,128)S(1)} %broadcast_in_dim.6), channel_id=1, replica_groups=mesh['y'=4,'x'=4,'z'=8,'core'=2] {'z'}, dimensions={0} | all-to-all | bytes 131072 | tf_op jit(solution)/shard_map/all_to_all | solution.py:163
  33.6 10.0 %all_to_all.17 = f32[16,16,128]{2,1,0:T(8,128)S(1)} all-to-all(f32[16,16,128]{2,1,0:T(8,128)S(1)} %broadcast_in_dim.7), channel_id=1, replica_groups=mesh['y'=4,'x'=4,'z'=8,'core'=2] {'y','x'}, dimensions={0} | all-to-all | bytes 262144 | tf_op jit(solution)/shard_map/all_to_all | solution.py:163
  43.7 0.0 copy-start
  43.7 4.3 %collective-permute-start.1 = (f32[256,128]{1,0:T(8,128)S(1)}, f32[256,128]{1,0:T(8,128)S(1)}, u32[]{:S(2)}, u32[]{:S(2)}) collective-permute-start(f32[256,128]{1,0:T(8,128)S(1)} %bitcast.16), channel_id=1, source_target_pairs={{0,1},{1,0},{2,3},{3,2},{4,5},{5,4},{6,7},{7,6},{8,9},{9,8},{10,11... | collective-permute-start | bytes 393224 | tf_op jit(solution)/shard_map/ppermute | solution.py:159
  47.9 1.0 %collective-permute-done.1.other_ref = f32[256,128]{1,0:T(8,128)S(1)} collective-permute-done((f32[256,128]{1,0:T(8,128)S(1)}, f32[256,128]{1,0:T(8,128)S(1)}, u32[]{:S(2)}, u32[]{:S(2)}) %collective-permute-start.1) | collective-permute-done | bytes 131104 | tf_op jit(solution)/shard_map/ppermute | solution.py:159
  48.9 0.0 copy-start.1
  48.9 0.0 copy-done
  48.9 0.6 copy-done.1
  49.6 19.3 %algebra.1 = (f32[128,1024]{1,0:T(8,128)}, f32[128,256]{1,0:T(8,128)}) custom-call(f32[256,128]{1,0:T(8,128)} %bitcast.17, f32[256,128]{1,0:T(8,128)} %copy-done.1, s32[1,1]{1,0:T(1,128)} %bitcast.6.core_ref, bf16[128,256]{1,0:T(8,128)(2,1)} %sketch_ref.1, bf16[256,1024]{1,0:T(8,128)(2,1)} %anomalies_ref.1), custom_call_target="tpu_custom_call" | custom-call | tf_op jit(solution)/shard_map/algebra/pallas_call | solution.py:192
  (7 shorter events, 0.1 us)
Async XLA Ops:
  2.4 4.3 %collective-permute-start = (f32[256,128]{1,0:T(8,128)S(1)}, f32[256,128]{1,0:T(8,128)S(1)}, u32[]{:S(2)}, u32[]{:S(2)}) collective-permute-start(f32[256,128]{1,0:T(8,128)S(1)} %fusion.1), channel_id=1, source_target_pairs={{0,1},{1,0},{2,3},{3,2},{4,5},{5,4},{6,7},{7,6},{8,9},{9,8},{10,11... | collective-permute-start | bytes 393224 | tf_op jit(solution)/shard_map/ppermute | solution.py:159
  43.7 5.2 %copy-start = (f32[16,16,128]{2,1,0:T(8,128)}, f32[16,16,128]{2,1,0:T(8,128)S(1)}, u32[]{:S(2)}) copy-start(f32[16,16,128]{2,1,0:T(8,128)S(1)} %all_to_all.17) | copy-start | bytes 393220
  43.7 5.2 %collective-permute-start.1 = (f32[256,128]{1,0:T(8,128)S(1)}, f32[256,128]{1,0:T(8,128)S(1)}, u32[]{:S(2)}, u32[]{:S(2)}) collective-permute-start(f32[256,128]{1,0:T(8,128)S(1)} %bitcast.16), channel_id=1, source_target_pairs={{0,1},{1,0},{2,3},{3,2},{4,5},{5,4},{6,7},{7,6},{8,9},{9,8},{10,11... | collective-permute-start | bytes 393224 | tf_op jit(solution)/shard_map/ppermute | solution.py:159
  48.9 0.7 copy-start.1

commit v2 on v1

v2 whole, which is shorter than its diff:
```python
import functools

import jax
import jax.numpy as jnp
from jax import lax
from jax.experimental import pallas as pl
from jax.experimental.pallas import tpu as pltpu
from jax.sharding import Mesh
from jax.sharding import PartitionSpec as P

PLANE = ("y", "x")
CELL_AXES = ("y", "x", "z", "core")
RANK = 128
DAYS = 256
SUB = 8
PANEL = 16
NEAR = 1e-5
HIGHEST = lax.Precision.HIGHEST


def dot(a, b, dims=((1,), (0,))):
    return lax.dot_general(
        a, b, (dims, ((), ())), precision=HIGHEST, preferred_element_type=jnp.float32
    )


def dot_nt(a, b):
    return dot(a, b, ((1,), (1,)))


def pieces(a):
    high = a.astype(jnp.bfloat16)
    rest = a - high.astype(jnp.float32)
    middle = rest.astype(jnp.bfloat16)
    low = (rest - middle.astype(jnp.float32)).astype(jnp.bfloat16)
    return high, middle, low


def dot_right(a, split, dims=((1,), (0,))):
    high, middle, low = (
        lax.dot_general(a, b, (dims, ((), ())), preferred_element_type=jnp.float32) for b in split
    )
    return high + (middle + low)


def dot_left(split, b, dims=((1,), (0,))):
    high, middle, low = (
        lax.dot_general(a, b, (dims, ((), ())), preferred_element_type=jnp.float32) for a in split
    )
    return high + (middle + low)


def spread(a):
    return jnp.broadcast_to(a, (SUB, RANK))


def eliminated(gram):
    lane = lax.broadcasted_iota(jnp.int32, (SUB, RANK), 1)
    sub = lax.broadcasted_iota(jnp.int32, (SUB, RANK), 0)
    at = [sub == s for s in range(SUB)]
    count, tall = RANK // SUB, PANEL // SUB
    rows = [gram[SUB * b : SUB * (b + 1), :] for b in range(count)]
    scales = []
    for p in range(0, count, tall):
        j = SUB * p
        block = rows[p : p + tall]
        kept, scale = list(block), [jnp.ones((SUB, RANK), jnp.float32)] * tall
        columns = [[spread(a[:, j + u : j + u + 1]) for a in block] for u in range(PANEL)]
        pivot = spread(columns[0][0][0:1, :])
        for t in range(PANEL):
            own, s = divmod(t, SUB)
            inverse = 1.0 / pivot
            scale[own] = jnp.where(at[s], pivot, scale[own])
            across = {v: spread(columns[v][own][s : s + 1, :]) for v in range(t + 1, PANEL)}
            if t + 1 < PANEL:
                b, r = divmod(t + 1, SUB)
                corner = spread(columns[t + 1][b][r : r + 1, :])
                pivot = corner - (across[t + 1] * across[t + 1]) * inverse
            row = spread(block[own][s : s + 1, :])
            kept[own] = jnp.where(at[s], row, kept[own])
            here = lane == j + t
            row = jnp.where(here, 1.0, row)
            for k in range(tall):
                changed = jnp.where(here, 0.0, block[k]) - (columns[t][k] * row) * inverse
                block[k] = jnp.where(at[s], row * inverse, changed) if k == own else changed
            for v in range(t + 1, PANEL):
                for k in range(tall):
                    changed = columns[v][k] - (columns[t][k] * across[v]) * inverse
                    if k == own:
                        changed = jnp.where(at[s], across[v] * inverse, changed)
                    columns[v][k] = changed
        rows[p : p + tall] = kept
        scales += scale
        solved = [spread(block[u // SUB][u % SUB : u % SUB + 1, :]) for u in range(PANEL)]
        inside = (lane >= j) & (lane < j + PANEL)
        for i in range(p + tall, count):
            terms = [spread(rows[i][:, j + u : j + u + 1]) * solved[u] for u in range(PANEL)]
            while len(terms) > 1:
                terms = [terms[k] + terms[k + 1] for k in range(0, len(terms), 2)]
            rows[i] = jnp.where(inside, 0.0, rows[i]) - terms[0]
    out = []
    for b in range(count):
        place = lane - (sub + SUB * b)
        unit = jnp.where(place < 0, rows[b], jnp.where(place == 0, 1.0, 0.0))
        out.append(unit * lax.rsqrt(scales[b]))
    return jnp.concatenate(out, axis=0)


def half_lower(a, row, column):
    return jnp.where(row > column, a, jnp.where(row == column, 0.5 * a, 0.0))


def correction(gram, out_ref):
    row = lax.broadcasted_iota(jnp.int32, (RANK, RANK), 0)
    column = lax.broadcasted_iota(jnp.int32, (RANK, RANK), 1)
    identity = jnp.where(row == column, 1.0, 0.0)
    error = gram - identity
    near = jnp.sum(error * error) < NEAR

    @pl.when(near)
    def _():
        first = half_lower(error, row, column)
        small = first.astype(jnp.bfloat16)
        square = jnp.dot(small, small, preferred_element_type=jnp.float32)
        outer = lax.dot_general(
            small, small, (((1,), (1,)), ((), ())), preferred_element_type=jnp.float32
        )
        out_ref[...] = (square + half_lower(outer, row, column)) - first

    @pl.when(jnp.logical_not(near))
    def _():
        out_ref[...] = eliminated(gram) - identity


def two(a):
    high = a.astype(jnp.bfloat16)
    return high, (a - high.astype(jnp.float32)).astype(jnp.bfloat16)


def corrected(change, array):
    change_high, change_low = change
    high, low = two(array)
    product = functools.partial(jnp.dot, preferred_element_type=jnp.float32)
    return array + (
        product(change_high, high) + (product(change_high, low) + product(change_low, high))
    )


def algebra(cells, mine_ref, other_ref, core_ref, sketch_ref, anomalies_ref, eofs_ref, pcs_ref, change_ref):
    first_core = core_ref[0, 0] == 0
    mine, other = mine_ref[...], other_ref[...]
    covariance = jnp.concatenate(
        [jnp.where(first_core, mine, other), jnp.where(first_core, other, mine)], axis=1
    )
    parts = pieces(covariance)
    sketch = sketch_ref[...]
    seen = dot_right(sketch, parts)
    gram = dot_left(pieces(seen), sketch, ((1,), (1,)))
    inverse = eliminated(gram)
    days = dot(inverse, seen)
    correction(dot_nt(days, dot_left(pieces(inverse), sketch)), change_ref)
    back = corrected(two(change_ref[...]), days).astype(jnp.bfloat16)
    gram = dot_left(pieces(dot_right(back, parts)), back, ((1,), (1,)))
    inverse = eliminated(gram)
    rows = dot_left(pieces(inverse), back)
    days = dot(rows, covariance)
    patterns = dot_left(pieces(rows), anomalies_ref[...])
    correction(dot_nt(days, rows), change_ref)
    change = two(change_ref[...])
    pcs_ref[...] = corrected(change, days) * jnp.sqrt(jnp.float32(DAYS) / jnp.float32(cells))
    eofs_ref[...] = corrected(change, patterns) * jnp.sqrt(jnp.float32(cells))


def exchanged(array):
    return lax.ppermute(array, "core", [(0, 1), (1, 0)])


def all_to_all(array, axes):
    return lax.all_to_all(array, axes, split_axis=0, concat_axis=0, tiled=True)


def sent_to_all(array, axes):
    return all_to_all(jnp.broadcast_to(array, (lax.axis_size(axes), *array.shape)), axes)


def summed_halves(anomalies):
    core = lax.axis_index("core")
    product = lax.dot_general(
        anomalies, anomalies, (((1,), (1,)), ((), ())), preferred_element_type=jnp.float32
    )
    halves = jnp.stack([product[:, :RANK], product[:, RANK:]])
    own = lax.dynamic_index_in_dim(halves, core, 0, False)
    partner = lax.dynamic_index_in_dim(halves, 1 - core, 0, False)
    half = own + exchanged(partner)
    count = lax.axis_size(PLANE)
    share = all_to_all(half.reshape(count, -1, RANK), PLANE).sum(axis=0)
    share = sent_to_all(share, "z").sum(axis=0)
    return sent_to_all(share, PLANE).reshape(DAYS, RANK)


def local(anomalies, sketch):
    mine = summed_halves(anomalies)
    other = exchanged(mine)
    core = lax.axis_index("core").astype(jnp.int32).reshape(1, 1)
    cells = anomalies.shape[1] * lax.axis_size(CELL_AXES)
    vmem = pl.BlockSpec(memory_space=pltpu.VMEM)
    smem = pl.BlockSpec(memory_space=pltpu.SMEM)
    return pl.pallas_call(
        functools.partial(algebra, cells),
        out_shape=(
            jax.ShapeDtypeStruct((RANK, anomalies.shape[1]), jnp.float32),
            jax.ShapeDtypeStruct((RANK, DAYS), jnp.float32),
        ),
        in_specs=[vmem, vmem, smem, vmem, vmem],
        out_specs=(vmem, vmem),
        scratch_shapes=[pltpu.VMEM((RANK, RANK), jnp.float32)],
        compiler_params=pltpu.CompilerParams(vmem_limit_bytes=16 * 2**20),
        name="algebra",
    )(mine, other, core, sketch, anomalies)


def solution(mesh):
    split = Mesh(mesh.devices.reshape(4, 4, 8, 2), CELL_AXES)
    in_specs = (P(None, CELL_AXES), P())
    out_specs = (P(None, CELL_AXES), P())
    return jax.shard_map(local, mesh=split, in_specs=in_specs, out_specs=out_specs, check_vma=False)
```

time: 69.1 us -> 61.1 us (0.88)
  Pallas kernels: 19.3 us -> 11.6 us
    pallas_call x1, Pallas kernels: 19.3 us -> 11.6 us  [local(): pl.pallas_call(functools.partial(algebra, cells), out_shape=(jax.ShapeDty...]
where the time goes in v2:
time: 61.1 us; the launch traced here: 60.8 us
  blocking collectives  37.2 us (61%)
  Pallas kernels  11.6 us (19%)
  starting transfers between devices  7.54 us (12%)
  waiting for transfers between devices  1.97 us (3%)
  matrix products  1.6 us (3%)
  between operations  0.7 us (1%)
    all_to_all x3, blocking collectives, all_to_all(): return lax.all_to_all(array, axes, split_axis=0, concat_axis=0, tiled=True)  37.2 us
    pallas_call x1, Pallas kernels, local(): pl.pallas_call(functools.partial(algebra, cells), out_shape=(jax.ShapeDty...  11.6 us
    ppermute x2, starting transfers between devices, exchanged(): return lax.ppermute(array, 'core', [(0, 1), (1, 0)])  7.54 us
    ppermute x2, waiting for transfers between devices, exchanged(): return lax.ppermute(array, 'core', [(0, 1), (1, 0)])  1.97 us
    dot_general x1, matrix products, summed_halves(): lax.dot_general(anomalies, anomalies, (((1,), (1,)), ((), ())), preferred...  1.6 us
  transfers between devices with their start and end apart: 2, of which 2 were waited for; matrix products, arithmetic and copies ran while one was open for 0% of the time, Pallas kernels for 0%

profile of v2, /device:TPU:1, one launch (start us, length us, event | category | flops | bytes accessed | tf_op | source)
XLA Modules:
  0.0 60.8 jit_solution(17384818488272298725)
XLA Ops:
  0.6 1.6 %fusion.5 = f32[256,256]{1,0:T(8,128)S(1)} fusion(bf16[256,1024]{1,0:T(8,128)(2,1)} %anomalies_ref.1), kind=kOutput, calls=%fused_computation.11 | convolution fusion | flops 134217728 | bytes 786432 | tf_op jit(solution)/shard_map/dot_general | solution.py:188
  2.3 3.3 %collective-permute-start = (f32[256,128]{1,0:T(8,128)S(1)}, f32[256,128]{1,0:T(8,128)S(1)}, u32[]{:S(2)}, u32[]{:S(2)}) collective-permute-start(f32[256,128]{1,0:T(8,128)S(1)} %fusion.1), channel_id=1, source_target_pairs={{0,1},{1,0},{2,3},{3,2},{4,5},{5,4},{6,7},{7,6},{8,9},{9,8},{10,11... | collective-permute-start | bytes 393224 | tf_op jit(solution)/shard_map/ppermute | solution.py:175
  5.6 1.0 %collective-permute-done = f32[256,128]{1,0:T(8,128)S(1)} collective-permute-done((f32[256,128]{1,0:T(8,128)S(1)}, f32[256,128]{1,0:T(8,128)S(1)}, u32[]{:S(2)}, u32[]{:S(2)}) %collective-permute-start) | collective-permute-done | bytes 131104 | tf_op jit(solution)/shard_map/ppermute | solution.py:175
  6.6 0.0 copy-start
  6.6 11.8 %all_to_all.15 = f32[16,16,128]{2,1,0:T(8,128)S(1)} all-to-all(f32[16,16,128]{2,1,0:T(8,128)S(1)} %bitcast.17), channel_id=1, replica_groups=mesh['y'=4,'x'=4,'z'=8,'core'=2] {'y','x'}, dimensions={0} | all-to-all | bytes 262144 | tf_op jit(solution)/shard_map/all_to_all | solution.py:179
  18.5 15.2 %all_to_all.16 = f32[8,16,128]{2,1,0:T(8,128)S(1)} all-to-all(f32[8,16,128]{2,1,0:T(8,128)S(1)} %broadcast_in_dim.6), channel_id=1, replica_groups=mesh['y'=4,'x'=4,'z'=8,'core'=2] {'z'}, dimensions={0} | all-to-all | bytes 131072 | tf_op jit(solution)/shard_map/all_to_all | solution.py:179
  33.7 0.0 copy-start.1
  33.7 10.2 %all_to_all.17 = f32[16,16,128]{2,1,0:T(8,128)S(1)} all-to-all(f32[16,16,128]{2,1,0:T(8,128)S(1)} %broadcast_in_dim.7), channel_id=1, replica_groups=mesh['y'=4,'x'=4,'z'=8,'core'=2] {'y','x'}, dimensions={0} | all-to-all | bytes 262144 | tf_op jit(solution)/shard_map/all_to_all | solution.py:179
  43.9 4.3 %collective-permute-start.1 = (f32[256,128]{1,0:T(8,128)S(1)}, f32[256,128]{1,0:T(8,128)S(1)}, u32[]{:S(2)}, u32[]{:S(2)}) collective-permute-start(f32[256,128]{1,0:T(8,128)S(1)} %bitcast.15), channel_id=1, source_target_pairs={{0,1},{1,0},{2,3},{3,2},{4,5},{5,4},{6,7},{7,6},{8,9},{9,8},{10,11... | collective-permute-start | bytes 393224 | tf_op jit(solution)/shard_map/ppermute | solution.py:175
  48.2 1.0 %collective-permute-done.1.other_ref = f32[256,128]{1,0:T(8,128)S(1)} collective-permute-done((f32[256,128]{1,0:T(8,128)S(1)}, f32[256,128]{1,0:T(8,128)S(1)}, u32[]{:S(2)}, u32[]{:S(2)}) %collective-permute-start.1) | collective-permute-done | bytes 131104 | tf_op jit(solution)/shard_map/ppermute | solution.py:175
  49.2 0.0 copy-done
  49.2 0.0 copy-done.1
  49.2 11.6 %algebra.1 = (f32[128,1024]{1,0:T(8,128)}, f32[128,256]{1,0:T(8,128)}) custom-call(f32[256,128]{1,0:T(8,128)S(1)} %bitcast.16, f32[256,128]{1,0:T(8,128)S(1)} %collective-permute-done.1.other_ref, s32[1,1]{1,0:T(1,128)} %bitcast.6.core_ref, bf16[128,256]{1,0:T(8,128)(2,1)S(1)} %copy-done.1, bf16[256,1024]{1,0:T(8,128)(2,1)S(1)} %copy-done), custom_call_target="tpu_custom_call" | custom-call | tf_op jit(solution)/shard_map/algebra/pallas_call | solution.py:208
  (7 shorter events, 0.1 us)
Async XLA Ops:
  2.3 4.3 %collective-permute-start = (f32[256,128]{1,0:T(8,128)S(1)}, f32[256,128]{1,0:T(8,128)S(1)}, u32[]{:S(2)}, u32[]{:S(2)}) collective-permute-start(f32[256,128]{1,0:T(8,128)S(1)} %fusion.1), channel_id=1, source_target_pairs={{0,1},{1,0},{2,3},{3,2},{4,5},{5,4},{6,7},{7,6},{8,9},{9,8},{10,11... | collective-permute-start | bytes 393224 | tf_op jit(solution)/shard_map/ppermute | solution.py:175
  6.6 42.5 %copy-start = (bf16[256,1024]{1,0:T(8,128)(2,1)S(1)}, bf16[256,1024]{1,0:T(8,128)(2,1)}, u32[]{:S(2)}) copy-start(bf16[256,1024]{1,0:T(8,128)(2,1)} %anomalies_ref.1) | copy-start | bytes 1572868
  33.7 15.4 %copy-start.1 = (bf16[128,256]{1,0:T(8,128)(2,1)S(1)}, bf16[128,256]{1,0:T(8,128)(2,1)}, u32[]{:S(2)}) copy-start(bf16[128,256]{1,0:T(8,128)(2,1)} %sketch_ref.1) | copy-start | bytes 196612
  43.9 5.2 %collective-permute-start.1 = (f32[256,128]{1,0:T(8,128)S(1)}, f32[256,128]{1,0:T(8,128)S(1)}, u32[]{:S(2)}, u32[]{:S(2)}) collective-permute-start(f32[256,128]{1,0:T(8,128)S(1)} %bitcast.15), channel_id=1, source_target_pairs={{0,1},{1,0},{2,3},{3,2},{4,5},{5,4},{6,7},{7,6},{8,9},{9,8},{10,11... | collective-permute-start | bytes 393224 | tf_op jit(solution)/shard_map/ppermute | solution.py:175

commit v3 on v2

--- a/solution.py
+++ b/solution.py
@@ -8,13 +8,15 @@
 from jax.sharding import Mesh
 from jax.sharding import PartitionSpec as P
 
-PLANE = ("y", "x")
+LAYER = ("y", "x", "core")
 CELL_AXES = ("y", "x", "z", "core")
 RANK = 128
 DAYS = 256
+PRODUCT_VMEM = 8 * 2**20
+PACKED = 288
 SUB = 8
 PANEL = 16
-NEAR = 1e-5
+NEAR = 2e-5
 HIGHEST = lax.Precision.HIGHEST
 
 
@@ -106,30 +108,48 @@
     return jnp.concatenate(out, axis=0)
 
 
-def half_lower(a, row, column):
+def eliminated_slowly(gram):
+    row = lax.broadcasted_iota(jnp.int32, (RANK, RANK), 0)
+    column = lax.broadcasted_iota(jnp.int32, (RANK, RANK), 1)
+
+    def step(j, a):
+        across = jnp.sum(jnp.where(row == j, a, 0.0), axis=0, keepdims=True)
+        down = jnp.sum(jnp.where(column == j, a, 0.0), axis=1, keepdims=True)
+        pivot = jnp.sum(jnp.where(column == row, jnp.where(row == j, a, 0.0), 0.0))
+        across = jnp.where(column == j, 1.0, across) / pivot
+        return jnp.where(row > j, jnp.where(column == j, 0.0, a) - down * across, a)
+
+    a = lax.fori_loop(0, RANK, step, gram)
+    pivots = jnp.sum(jnp.where(row == column, a, 0.0), axis=1, keepdims=True)
+    unit = jnp.where(row > column, a, jnp.where(row == column, 1.0, 0.0))
+    return unit * lax.rsqrt(pivots)
+
+
+def identity():
+    row = lax.broadcasted_iota(jnp.int32, (RANK, RANK), 0)
+    column = lax.broadcasted_iota(jnp.int32, (RANK, RANK), 1)
+    return jnp.where(row == column, 1.0, 0.0)
+
+
+def half_lower(a):
+    row = lax.broadcasted_iota(jnp.int32, (RANK, RANK), 0)
+    column = lax.broadcasted_iota(jnp.int32, (RANK, RANK), 1)
     return jnp.where(row > column, a, jnp.where(row == column, 0.5 * a, 0.0))
 
 
-def correction(gram, out_ref):
-    row = lax.broadcasted_iota(jnp.int32, (RANK, RANK), 0)
-    column = lax.broadcasted_iota(jnp.int32, (RANK, RANK), 1)
-    identity = jnp.where(row == column, 1.0, 0.0)
-    error = gram - identity
-    near = jnp.sum(error * error) < NEAR
-
-    @pl.when(near)
-    def _():
-        first = half_lower(error, row, column)
-        small = first.astype(jnp.bfloat16)
-        square = jnp.dot(small, small, preferred_element_type=jnp.float32)
-        outer = lax.dot_general(
-            small, small, (((1,), (1,)), ((), ())), preferred_element_type=jnp.float32
-        )
-        out_ref[...] = (square + half_lower(outer, row, column)) - first
-
-    @pl.when(jnp.logical_not(near))
-    def _():
-        out_ref[...] = eliminated(gram) - identity
+def series(gram):
+    error = gram - identity()
+    first = half_lower(error)
+    small = first.astype(jnp.bfloat16)
+    square = jnp.dot(small, small, preferred_element_type=jnp.float32)
+    outer = lax.dot_general(
+        small, small, (((1,), (1,)), ((), ())), preferred_element_type=jnp.float32
+    )
+    return (square + half_lower(outer)) - first, jnp.sum(error * error)
+
+
+def whole(gram):
+    return eliminated_slowly(gram) - identity(), None
 
 
 def two(a):
@@ -146,33 +166,67 @@
     )
 
 
-def algebra(cells, mine_ref, other_ref, core_ref, sketch_ref, anomalies_ref, eofs_ref, pcs_ref, change_ref):
-    first_core = core_ref[0, 0] == 0
-    mine, other = mine_ref[...], other_ref[...]
-    covariance = jnp.concatenate(
-        [jnp.where(first_core, mine, other), jnp.where(first_core, other, mine)], axis=1
-    )
+def unpacked(packed):
+    row = lax.broadcasted_iota(jnp.int32, (RANK, RANK), 0)
+    column = lax.broadcasted_iota(jnp.int32, (RANK, RANK), 1)
+    corner, both = packed[:RANK, :], packed[RANK:DAYS, :]
+    flipped = both.T
+    diagonal = packed[DAYS : DAYS + 1, :]
+    first = jnp.where(row >= column, both, flipped)
+    last = jnp.where(row < column, both, jnp.where(row == column, diagonal, flipped))
+    return jnp.concatenate(
+        [jnp.concatenate([first, corner], axis=1), jnp.concatenate([corner.T, last], axis=1)],
+        axis=0,
+    )
+
+
+def outputs(cells, first_factor, second_factor, refs):
+    packed_ref, sketch_ref, anomalies_ref, eofs_ref, pcs_ref = refs
+    covariance = unpacked(packed_ref[...])
     parts = pieces(covariance)
     sketch = sketch_ref[...]
     seen = dot_right(sketch, parts)
     gram = dot_left(pieces(seen), sketch, ((1,), (1,)))
-    inverse = eliminated(gram)
+    inverse = first_factor(gram)
     days = dot(inverse, seen)
-    correction(dot_nt(days, dot_left(pieces(inverse), sketch)), change_ref)
-    back = corrected(two(change_ref[...]), days).astype(jnp.bfloat16)
+    change, first_error = second_factor(dot_nt(days, dot_left(pieces(inverse), sketch)))
+    back = corrected(two(change), days).astype(jnp.bfloat16)
     gram = dot_left(pieces(dot_right(back, parts)), back, ((1,), (1,)))
-    inverse = eliminated(gram)
+    inverse = first_factor(gram)
     rows = dot_left(pieces(inverse), back)
     days = dot(rows, covariance)
     patterns = dot_left(pieces(rows), anomalies_ref[...])
-    correction(dot_nt(days, rows), change_ref)
-    change = two(change_ref[...])
+    change, last_error = second_factor(dot_nt(days, rows))
+    change = two(change)
     pcs_ref[...] = corrected(change, days) * jnp.sqrt(jnp.float32(DAYS) / jnp.float32(cells))
     eofs_ref[...] = corrected(change, patterns) * jnp.sqrt(jnp.float32(cells))
-
-
-def exchanged(array):
-    return lax.ppermute(array, "core", [(0, 1), (1, 0)])
+    return first_error, last_error
+
+
+def algebra(cells, *refs):
+    first_error, last_error = outputs(cells, eliminated, series, refs)
+
+    @pl.when(jnp.logical_not((first_error < NEAR) & (last_error < NEAR)))
+    def _():
+        outputs(cells, eliminated_slowly, whole, refs)
+
+
+def product(anomalies_ref, packed_ref, here, arrived):
+    copy = pltpu.make_async_copy(anomalies_ref, here, arrived)
+    copy.start()
+    copy.wait()
+    cells = here[...]
+    total = lax.dot_general(
+        cells, cells, (((1,), (1,)), ((), ())), preferred_element_type=jnp.float32
+    )
+    row = lax.broadcasted_iota(jnp.int32, (RANK, RANK), 0)
+    column = lax.broadcasted_iota(jnp.int32, (RANK, RANK), 1)
+    first, last = total[:RANK, :RANK], total[RANK:, RANK:]
+    diagonal = jnp.sum(jnp.where(row == column, last, 0.0), axis=0, keepdims=True)
+    packed_ref[:RANK, :] = total[:RANK, RANK:]
+    packed_ref[RANK:DAYS, :] = jnp.where(row >= column, first, last)
+    spare = lax.broadcasted_iota(jnp.int32, (PACKED - DAYS, RANK), 0)
+    packed_ref[DAYS:, :] = jnp.where(spare == 0, diagonal, 0.0)
 
 
 def all_to_all(array, axes):
@@ -183,40 +237,36 @@
     return all_to_all(jnp.broadcast_to(array, (lax.axis_size(axes), *array.shape)), axes)
 
 
-def summed_halves(anomalies):
-    core = lax.axis_index("core")
-    product = lax.dot_general(
-        anomalies, anomalies, (((1,), (1,)), ((), ())), preferred_element_type=jnp.float32
-    )
-    halves = jnp.stack([product[:, :RANK], product[:, RANK:]])
-    own = lax.dynamic_index_in_dim(halves, core, 0, False)
-    partner = lax.dynamic_index_in_dim(halves, 1 - core, 0, False)
-    half = own + exchanged(partner)
-    count = lax.axis_size(PLANE)
-    share = all_to_all(half.reshape(count, -1, RANK), PLANE).sum(axis=0)
+def summed(packed):
+    shares = packed.reshape(lax.axis_size(LAYER), -1, 1, RANK)
+    share = all_to_all(shares, LAYER).sum(axis=0)
     share = sent_to_all(share, "z").sum(axis=0)
-    return sent_to_all(share, PLANE).reshape(DAYS, RANK)
+    return sent_to_all(share, LAYER).reshape(packed.shape)
 
 
 def local(anomalies, sketch):
-    mine = summed_halves(anomalies)
-    other = exchanged(mine)
-    core = lax.axis_index("core").astype(jnp.int32).reshape(1, 1)
     cells = anomalies.shape[1] * lax.axis_size(CELL_AXES)
     vmem = pl.BlockSpec(memory_space=pltpu.VMEM)
-    smem = pl.BlockSpec(memory_space=pltpu.SMEM)
+    packed = pl.pallas_call(
+        product,
+        out_shape=jax.ShapeDtypeStruct((PACKED, RANK), jnp.float32),
+        in_specs=[pl.BlockSpec(memory_space=pltpu.HBM)],
+        out_specs=vmem,
+        scratch_shapes=[pltpu.VMEM(anomalies.shape, anomalies.dtype), pltpu.SemaphoreType.DMA],
+        compiler_params=pltpu.CompilerParams(vmem_limit_bytes=PRODUCT_VMEM),
+        name="product",
+    )(pltpu.with_memory_space_constraint(anomalies, pltpu.HBM))
     return pl.pallas_call(
         functools.partial(algebra, cells),
         out_shape=(
             jax.ShapeDtypeStruct((RANK, anomalies.shape[1]), jnp.float32),
             jax.ShapeDtypeStruct((RANK, DAYS), jnp.float32),
         ),
-        in_specs=[vmem, vmem, smem, vmem, vmem],
+        in_specs=[vmem, vmem, vmem],
         out_specs=(vmem, vmem),
-        scratch_shapes=[pltpu.VMEM((RANK, RANK), jnp.float32)],
         compiler_params=pltpu.CompilerParams(vmem_limit_bytes=16 * 2**20),
         name="algebra",
-    )(mine, other, core, sketch, anomalies)
+    )(summed(packed), sketch, anomalies)
 
 
 def solution(mesh):

time: 61.1 us -> 57.9 us (0.948)
  starting transfers between devices: 7.54 us -> 0 us
  blocking collectives: 37.2 us -> 44.1 us
  waiting for transfers between devices: 1.97 us -> 0 us
  matrix products: 1.6 us -> 0 us
  Pallas kernels: 11.6 us -> 12.6 us
    ppermute x2 -> x0, starting transfers between devices: 7.54 us -> none  [exchanged(): return lax.ppermute(array, 'core', [(0, 1), (1, 0)])]
    all_to_all x3, blocking collectives: 37.2 us -> 44.1 us  [all_to_all(): return lax.all_to_all(array, axes, split_axis=0, concat_axis=0, tiled=True)]
    ppermute x2 -> x0, waiting for transfers between devices: 1.97 us -> none  [exchanged(): return lax.ppermute(array, 'core', [(0, 1), (1, 0)])]
    dot_general x1 -> x0, matrix products: 1.6 us -> none  [summed_halves(): lax.dot_general(anomalies, anomalies, (((1,), (1,)), ((), ())), preferred...]
    pallas_call x0 -> x1, Pallas kernels: none -> 1.4 us  [local(): pl.pallas_call(product, out_shape=jax.ShapeDtypeStruct((PACKED, RANK), jn...]
  transfers between devices with their start and end apart: 2 -> 0, of which waited for: 2 -> 0; matrix products, arithmetic and copies ran while one was open for 0% -> 0% of each run, Pallas kernels for 0% -> 0%
where the time goes in v3:
time: 57.9 us; the launch traced here: 57.7 us
  blocking collectives  44.1 us (76%)
  Pallas kernels  12.6 us (22%)
  between operations  0.68 us (1%)
    all_to_all x3, blocking collectives, all_to_all(): return lax.all_to_all(array, axes, split_axis=0, concat_axis=0, tiled=True)  44.1 us
    pallas_call x1, Pallas kernels, local(): pl.pallas_call(functools.partial(algebra, cells), out_shape=(jax.ShapeDty...  11.2 us
    pallas_call x1, Pallas kernels, local(): pl.pallas_call(product, out_shape=jax.ShapeDtypeStruct((PACKED, RANK), jn...  1.4 us

profile of v3, /device:TPU:1, one launch (start us, length us, event | category | flops | bytes accessed | tf_op | source)
XLA Modules:
  0.0 57.7 jit_solution(5709163426087785308)
XLA Ops:
  0.6 1.4 %product.1 = f32[288,128]{1,0:T(8,128)S(1)} custom-call(bf16[256,1024]{1,0:T(8,128)(2,1)} %refs_2_.1), custom_call_target="tpu_custom_call" | custom-call | tf_op jit(solution)/shard_map/product/pallas_call | solution.py:250
  2.0 0.0 copy-start
  2.0 16.3 %all_to_all.15 = f32[32,9,1,128]{3,2,1,0:T(1,128)S(1)} all-to-all(f32[32,9,1,128]{3,2,1,0:T(1,128)S(1)} %bitcast.3), channel_id=1, replica_groups=mesh['y'=4,'x'=4,'z'=8,'core'=2] {'y','x','core'}, dimensions={0} | all-to-all | bytes 294912 | tf_op jit(solution)/shard_map/all_to_all | solution.py:233
  18.3 0.1 reduce_sum.18
  18.4 15.0 %all_to_all.16 = f32[8,9,1,128]{3,2,1,0:T(1,128)S(1)} all-to-all(f32[8,9,1,128]{3,2,1,0:T(1,128)S(1)} %broadcast_in_dim.6), channel_id=1, replica_groups=mesh['y'=4,'x'=4,'z'=8,'core'=2] {'z'}, dimensions={0} | all-to-all | bytes 73728 | tf_op jit(solution)/shard_map/all_to_all | solution.py:233
  33.5 0.1 broadcast_in_dim.7
  33.5 0.0 copy-start.1
  33.6 12.9 %all_to_all.17 = f32[32,9,1,128]{3,2,1,0:T(1,128)S(1)} all-to-all(f32[32,9,1,128]{3,2,1,0:T(1,128)S(1)} %broadcast_in_dim.7), channel_id=1, replica_groups=mesh['y'=4,'x'=4,'z'=8,'core'=2] {'y','x','core'}, dimensions={0} | all-to-all | bytes 294912 | tf_op jit(solution)/shard_map/all_to_all | solution.py:233
  46.4 0.0 copy-done
  46.4 0.0 copy-done.1
  46.4 11.2 %algebra.1 = (f32[128,1024]{1,0:T(8,128)}, f32[128,256]{1,0:T(8,128)}) custom-call(f32[288,128]{1,0:T(8,128)S(1)} %bitcast.2, bf16[128,256]{1,0:T(8,128)(2,1)S(1)} %copy-done.1, bf16[256,1024]{1,0:T(8,128)(2,1)S(1)} %copy-done), custom_call_target="tpu_custom_call" | custom-call | tf_op jit(solution)/shard_map/algebra/pallas_call | solution.py:259
  (2 shorter events, 0.1 us)
Async XLA Ops:
  2.0 44.4 %copy-start = (bf16[256,1024]{1,0:T(8,128)(2,1)S(1)}, bf16[256,1024]{1,0:T(8,128)(2,1)}, u32[]{:S(2)}) copy-start(bf16[256,1024]{1,0:T(8,128)(2,1)} %refs_2_.1) | copy-start | bytes 1572868
  33.5 12.9 %copy-start.1 = (bf16[128,256]{1,0:T(8,128)(2,1)S(1)}, bf16[128,256]{1,0:T(8,128)(2,1)}, u32[]{:S(2)}) copy-start(bf16[128,256]{1,0:T(8,128)(2,1)} %refs_1_.1) | copy-start | bytes 196612

commit v4 on v3

--- a/solution.py
+++ b/solution.py
@@ -16,7 +16,7 @@
 PACKED = 288
 SUB = 8
 PANEL = 16
-NEAR = 2e-5
+NEAR = {1: 1e-7, 2: 2e-5}
 HIGHEST = lax.Precision.HIGHEST
 
 
@@ -81,16 +81,15 @@
             row = spread(block[own][s : s + 1, :])
             kept[own] = jnp.where(at[s], row, kept[own])
             here = lane == j + t
-            row = jnp.where(here, 1.0, row)
+            row = jnp.where(here, 1.0, row) * inverse
             for k in range(tall):
-                changed = jnp.where(here, 0.0, block[k]) - (columns[t][k] * row) * inverse
-                block[k] = jnp.where(at[s], row * inverse, changed) if k == own else changed
+                changed = jnp.where(here, 0.0, block[k]) - columns[t][k] * row
+                block[k] = jnp.where(at[s], row, changed) if k == own else changed
             for v in range(t + 1, PANEL):
+                ratio = across[v] * inverse
                 for k in range(tall):
-                    changed = columns[v][k] - (columns[t][k] * across[v]) * inverse
-                    if k == own:
-                        changed = jnp.where(at[s], across[v] * inverse, changed)
-                    columns[v][k] = changed
+                    changed = columns[v][k] - columns[t][k] * ratio
+                    columns[v][k] = jnp.where(at[s], ratio, changed) if k == own else changed
         rows[p : p + tall] = kept
         scales += scale
         solved = [spread(block[u // SUB][u % SUB : u % SUB + 1, :]) for u in range(PANEL)]
@@ -137,18 +136,21 @@
     return jnp.where(row > column, a, jnp.where(row == column, 0.5 * a, 0.0))
 
 
-def series(gram):
+def series(gram, order):
     error = gram - identity()
+    near = jnp.sum(error * error) < NEAR[order]
     first = half_lower(error)
+    if order == 1:
+        return -first, near
     small = first.astype(jnp.bfloat16)
     square = jnp.dot(small, small, preferred_element_type=jnp.float32)
     outer = lax.dot_general(
         small, small, (((1,), (1,)), ((), ())), preferred_element_type=jnp.float32
     )
-    return (square + half_lower(outer)) - first, jnp.sum(error * error)
-
-
-def whole(gram):
+    return (square + half_lower(outer)) - first, near
+
+
+def whole(gram, order):
     return eliminated_slowly(gram) - identity(), None
 
 
@@ -189,24 +191,25 @@
     gram = dot_left(pieces(seen), sketch, ((1,), (1,)))
     inverse = first_factor(gram)
     days = dot(inverse, seen)
-    change, first_error = second_factor(dot_nt(days, dot_left(pieces(inverse), sketch)))
+    change, first_near = second_factor(dot_nt(days, dot_left(pieces(inverse), sketch)), 1)
     back = corrected(two(change), days).astype(jnp.bfloat16)
-    gram = dot_left(pieces(dot_right(back, parts)), back, ((1,), (1,)))
+    seen = dot_right(back, parts)
+    gram = dot_left(pieces(seen), back, ((1,), (1,)))
     inverse = first_factor(gram)
     rows = dot_left(pieces(inverse), back)
-    days = dot(rows, covariance)
+    days = dot(inverse, seen)
     patterns = dot_left(pieces(rows), anomalies_ref[...])
-    change, last_error = second_factor(dot_nt(days, rows))
+    change, last_near = second_factor(dot_nt(days, rows), 2)
     change = two(change)
     pcs_ref[...] = corrected(change, days) * jnp.sqrt(jnp.float32(DAYS) / jnp.float32(cells))
     eofs_ref[...] = corrected(change, patterns) * jnp.sqrt(jnp.float32(cells))
-    return first_error, last_error
+    return first_near, last_near
 
 
 def algebra(cells, *refs):
-    first_error, last_error = outputs(cells, eliminated, series, refs)
-
-    @pl.when(jnp.logical_not((first_error < NEAR) & (last_error < NEAR)))
+    first_near, last_near = outputs(cells, eliminated, series, refs)
+
+    @pl.when(jnp.logical_not(first_near & last_near))
     def _():
         outputs(cells, eliminated_slowly, whole, refs)
 

time: 57.9 us -> 57.2 us (0.988)
  Pallas kernels: 12.6 us -> 11.9 us
    pallas_call x1, Pallas kernels: 11.2 us -> 10.5 us  [local(): pl.pallas_call(functools.partial(algebra, cells), out_shape=(jax.ShapeDty...]
where the time goes in v4:
time: 57.2 us; the launch traced here: 56.9 us
  blocking collectives  44.1 us (77%)
  Pallas kernels  11.9 us (21%)
  between operations  0.68 us (1%)
    all_to_all x3, blocking collectives, all_to_all(): return lax.all_to_all(array, axes, split_axis=0, concat_axis=0, tiled=True)  44.1 us
    pallas_call x1, Pallas kernels, local(): pl.pallas_call(functools.partial(algebra, cells), out_shape=(jax.ShapeDty...  10.5 us
    pallas_call x1, Pallas kernels, local(): pl.pallas_call(product, out_shape=jax.ShapeDtypeStruct((PACKED, RANK), jn...  1.4 us

profile of v4, /device:TPU:1, one launch (start us, length us, event | category | flops | bytes accessed | tf_op | source)
XLA Modules:
  0.0 56.9 jit_solution(2478940340872153746)
XLA Ops:
  0.6 1.4 %product.1 = f32[288,128]{1,0:T(8,128)S(1)} custom-call(bf16[256,1024]{1,0:T(8,128)(2,1)} %refs_2_.1), custom_call_target="tpu_custom_call" | custom-call | tf_op jit(solution)/shard_map/product/pallas_call | solution.py:253
  2.0 0.0 copy-start
  2.0 16.3 %all_to_all.15 = f32[32,9,1,128]{3,2,1,0:T(1,128)S(1)} all-to-all(f32[32,9,1,128]{3,2,1,0:T(1,128)S(1)} %bitcast.3), channel_id=1, replica_groups=mesh['y'=4,'x'=4,'z'=8,'core'=2] {'y','x','core'}, dimensions={0} | all-to-all | bytes 294912 | tf_op jit(solution)/shard_map/all_to_all | solution.py:236
  18.3 0.1 reduce_sum.18
  18.4 15.0 %all_to_all.16 = f32[8,9,1,128]{3,2,1,0:T(1,128)S(1)} all-to-all(f32[8,9,1,128]{3,2,1,0:T(1,128)S(1)} %broadcast_in_dim.6), channel_id=1, replica_groups=mesh['y'=4,'x'=4,'z'=8,'core'=2] {'z'}, dimensions={0} | all-to-all | bytes 73728 | tf_op jit(solution)/shard_map/all_to_all | solution.py:236
  33.5 0.1 broadcast_in_dim.7
  33.5 0.0 copy-start.1
  33.6 12.9 %all_to_all.17 = f32[32,9,1,128]{3,2,1,0:T(1,128)S(1)} all-to-all(f32[32,9,1,128]{3,2,1,0:T(1,128)S(1)} %broadcast_in_dim.7), channel_id=1, replica_groups=mesh['y'=4,'x'=4,'z'=8,'core'=2] {'y','x','core'}, dimensions={0} | all-to-all | bytes 294912 | tf_op jit(solution)/shard_map/all_to_all | solution.py:236
  46.4 0.0 copy-done
  46.4 0.0 copy-done.1
  46.4 10.5 %algebra.1 = (f32[128,1024]{1,0:T(8,128)}, f32[128,256]{1,0:T(8,128)}) custom-call(f32[288,128]{1,0:T(8,128)S(1)} %bitcast.2, bf16[128,256]{1,0:T(8,128)(2,1)S(1)} %copy-done.1, bf16[256,1024]{1,0:T(8,128)(2,1)S(1)} %copy-done), custom_call_target="tpu_custom_call" | custom-call | tf_op jit(solution)/shard_map/algebra/pallas_call | solution.py:262
  (2 shorter events, 0.1 us)
Async XLA Ops:
  2.0 44.4 %copy-start = (bf16[256,1024]{1,0:T(8,128)(2,1)S(1)}, bf16[256,1024]{1,0:T(8,128)(2,1)}, u32[]{:S(2)}) copy-start(bf16[256,1024]{1,0:T(8,128)(2,1)} %refs_2_.1) | copy-start | bytes 1572868
  33.5 12.9 %copy-start.1 = (bf16[128,256]{1,0:T(8,128)(2,1)S(1)}, bf16[128,256]{1,0:T(8,128)(2,1)}, u32[]{:S(2)}) copy-start(bf16[128,256]{1,0:T(8,128)(2,1)} %refs_1_.1) | copy-start | bytes 196612

commit v5 on v4

--- a/solution.py
+++ b/solution.py
@@ -62,6 +62,7 @@
     at = [sub == s for s in range(SUB)]
     count, tall = RANK // SUB, PANEL // SUB
     rows = [gram[SUB * b : SUB * (b + 1), :] for b in range(count)]
+    zeros = jnp.zeros((SUB, RANK), jnp.float32)
     scales = []
     for p in range(0, count, tall):
         j = SUB * p
@@ -92,13 +93,26 @@
                     columns[v][k] = jnp.where(at[s], ratio, changed) if k == own else changed
         rows[p : p + tall] = kept
         scales += scale
-        solved = [spread(block[u // SUB][u % SUB : u % SUB + 1, :]) for u in range(PANEL)]
         inside = (lane >= j) & (lane < j + PANEL)
-        for i in range(p + tall, count):
-            terms = [spread(rows[i][:, j + u : j + u + 1]) * solved[u] for u in range(PANEL)]
-            while len(terms) > 1:
-                terms = [terms[k] + terms[k + 1] for k in range(0, len(terms), 2)]
-            rows[i] = jnp.where(inside, 0.0, rows[i]) - terms[0]
+        behind = p + 2 * tall
+        if p + tall < count:
+            solved = [spread(block[u // SUB][u % SUB : u % SUB + 1, :]) for u in range(PANEL)]
+            terms = {
+                i: [spread(rows[i][:, j + u : j + u + 1]) * solved[u] for u in range(PANEL)]
+                for i in range(p + tall, behind)
+            }
+            for i, total in terms.items():
+                while len(total) > 1:
+                    total = [total[k] + total[k + 1] for k in range(0, len(total), 2)]
+                rows[i] = jnp.where(inside, 0.0, rows[i]) - total[0]
+        if behind < count:
+            across_panel = jnp.concatenate(
+                [zeros] * p + block + [zeros] * (count - p - tall), axis=0
+            )
+            total = dot(jnp.concatenate(rows[behind:], axis=0), across_panel)
+            for i in range(behind, count):
+                k = SUB * (i - behind)
+                rows[i] = jnp.where(inside, 0.0, rows[i]) - total[k : k + SUB, :]
     out = []
     for b in range(count):
         place = lane - (sub + SUB * b)
@@ -159,10 +173,12 @@
     return high, (a - high.astype(jnp.float32)).astype(jnp.bfloat16)
 
 
-def corrected(change, array):
-    change_high, change_low = change
+def corrected(change, array, small):
+    product = functools.partial(jnp.dot, preferred_element_type=jnp.float32)
+    if small:
+        return array + product(change.astype(jnp.bfloat16), array.astype(jnp.bfloat16))
+    change_high, change_low = two(change)
     high, low = two(array)
-    product = functools.partial(jnp.dot, preferred_element_type=jnp.float32)
     return array + (
         product(change_high, high) + (product(change_high, low) + product(change_low, high))
     )
@@ -192,17 +208,19 @@
     inverse = first_factor(gram)
     days = dot(inverse, seen)
     change, first_near = second_factor(dot_nt(days, dot_left(pieces(inverse), sketch)), 1)
-    back = corrected(two(change), days).astype(jnp.bfloat16)
+    small = second_factor is series
+    back = corrected(change, days, small).astype(jnp.bfloat16)
     seen = dot_right(back, parts)
     gram = dot_left(pieces(seen), back, ((1,), (1,)))
     inverse = first_factor(gram)
     rows = dot_left(pieces(inverse), back)
     days = dot(inverse, seen)
-    patterns = dot_left(pieces(rows), anomalies_ref[...])
+    scale = jnp.sqrt(jnp.float32(cells))
+    patterns = dot_left(pieces(rows * scale), anomalies_ref[...])
     change, last_near = second_factor(dot_nt(days, rows), 2)
-    change = two(change)
-    pcs_ref[...] = corrected(change, days) * jnp.sqrt(jnp.float32(DAYS) / jnp.float32(cells))
-    eofs_ref[...] = corrected(change, patterns) * jnp.sqrt(jnp.float32(cells))
+    day_scale = jnp.sqrt(jnp.float32(DAYS) / jnp.float32(cells))
+    pcs_ref[...] = corrected(change, days, small) * day_scale
+    eofs_ref[...] = corrected(change, patterns, small)
     return first_near, last_near
 
 

time: 57.2 us -> 55.3 us (0.967)
  Pallas kernels: 11.9 us -> 9.97 us
    pallas_call x1, Pallas kernels: 10.5 us -> 8.57 us  [local(): pl.pallas_call(functools.partial(algebra, cells), out_shape=(jax.ShapeDty...]
where the time goes in v5:
time: 55.3 us; the launch traced here: 55 us
  blocking collectives  44.1 us (80%)
  Pallas kernels  9.97 us (18%)
  between operations  0.68 us (1%)
    all_to_all x3, blocking collectives, all_to_all(): return lax.all_to_all(array, axes, split_axis=0, concat_axis=0, tiled=True)  44.1 us
    pallas_call x1, Pallas kernels, local(): pl.pallas_call(functools.partial(algebra, cells), out_shape=(jax.ShapeDty...  8.57 us
    pallas_call x1, Pallas kernels, local(): pl.pallas_call(product, out_shape=jax.ShapeDtypeStruct((PACKED, RANK), jn...  1.4 us

profile of v5, /device:TPU:1, one launch (start us, length us, event | category | flops | bytes accessed | tf_op | source)
XLA Modules:
  0.0 55.0 jit_solution(14750071046051615078)
XLA Ops:
  0.6 1.4 %product.1 = f32[288,128]{1,0:T(8,128)S(1)} custom-call(bf16[256,1024]{1,0:T(8,128)(2,1)} %refs_2_.1), custom_call_target="tpu_custom_call" | custom-call | tf_op jit(solution)/shard_map/product/pallas_call | solution.py:271
  2.0 0.0 copy-start
  2.0 16.3 %all_to_all.15 = f32[32,9,1,128]{3,2,1,0:T(1,128)S(1)} all-to-all(f32[32,9,1,128]{3,2,1,0:T(1,128)S(1)} %bitcast.3), channel_id=1, replica_groups=mesh['y'=4,'x'=4,'z'=8,'core'=2] {'y','x','core'}, dimensions={0} | all-to-all | bytes 294912 | tf_op jit(solution)/shard_map/all_to_all | solution.py:254
  18.3 0.1 reduce_sum.18
  18.4 15.0 %all_to_all.16 = f32[8,9,1,128]{3,2,1,0:T(1,128)S(1)} all-to-all(f32[8,9,1,128]{3,2,1,0:T(1,128)S(1)} %broadcast_in_dim.6), channel_id=1, replica_groups=mesh['y'=4,'x'=4,'z'=8,'core'=2] {'z'}, dimensions={0} | all-to-all | bytes 73728 | tf_op jit(solution)/shard_map/all_to_all | solution.py:254
  33.5 0.1 broadcast_in_dim.7
  33.5 0.0 copy-start.1
  33.6 12.9 %all_to_all.17 = f32[32,9,1,128]{3,2,1,0:T(1,128)S(1)} all-to-all(f32[32,9,1,128]{3,2,1,0:T(1,128)S(1)} %broadcast_in_dim.7), channel_id=1, replica_groups=mesh['y'=4,'x'=4,'z'=8,'core'=2] {'y','x','core'}, dimensions={0} | all-to-all | bytes 294912 | tf_op jit(solution)/shard_map/all_to_all | solution.py:254
  46.4 0.0 copy-done
  46.4 0.0 copy-done.1
  46.4 8.6 %algebra.1 = (f32[128,1024]{1,0:T(8,128)}, f32[128,256]{1,0:T(8,128)}) custom-call(f32[288,128]{1,0:T(8,128)S(1)} %bitcast.2, bf16[128,256]{1,0:T(8,128)(2,1)S(1)} %copy-done.1, bf16[256,1024]{1,0:T(8,128)(2,1)S(1)} %copy-done), custom_call_target="tpu_custom_call" | custom-call | tf_op jit(solution)/shard_map/algebra/pallas_call | solution.py:280
  (2 shorter events, 0.1 us)
Async XLA Ops:
  2.0 44.4 %copy-start = (bf16[256,1024]{1,0:T(8,128)(2,1)S(1)}, bf16[256,1024]{1,0:T(8,128)(2,1)}, u32[]{:S(2)}) copy-start(bf16[256,1024]{1,0:T(8,128)(2,1)} %refs_2_.1) | copy-start | bytes 1572868
  33.5 12.9 %copy-start.1 = (bf16[128,256]{1,0:T(8,128)(2,1)S(1)}, bf16[128,256]{1,0:T(8,128)(2,1)}, u32[]{:S(2)}) copy-start(bf16[128,256]{1,0:T(8,128)(2,1)} %refs_1_.1) | copy-start | bytes 196612

commit v6 on v5

--- a/solution.py
+++ b/solution.py
@@ -8,7 +8,7 @@
 from jax.sharding import Mesh
 from jax.sharding import PartitionSpec as P
 
-LAYER = ("y", "x", "core")
+LAYER = ("y", "x")
 CELL_AXES = ("y", "x", "z", "core")
 RANK = 128
 DAYS = 256
@@ -259,8 +259,9 @@
 
 
 def summed(packed):
-    shares = packed.reshape(lax.axis_size(LAYER), -1, 1, RANK)
+    shares = packed.reshape(lax.axis_size(LAYER), -1, 2, RANK)
     share = all_to_all(shares, LAYER).sum(axis=0)
+    share = share + lax.ppermute(share, "core", [(0, 1), (1, 0)])
     share = sent_to_all(share, "z").sum(axis=0)
     return sent_to_all(share, LAYER).reshape(packed.shape)
 

time: 55.3 us -> 54.3 us (0.982)
  the two profiles are of different devices: /device:TPU:1 before, /device:TPU:2 now
where the time goes in v6:
time: 54.3 us; the launch traced here: 54 us
  blocking collectives  42 us (77%)
  Pallas kernels  9.97 us (18%)
  waiting for transfers between devices  1.16 us (2%)
  between operations  0.67 us (1%)
    all_to_all x3, blocking collectives, all_to_all(): return lax.all_to_all(array, axes, split_axis=0, concat_axis=0, tiled=True)  42 us
    pallas_call x1, Pallas kernels, local(): pl.pallas_call(functools.partial(algebra, cells), out_shape=(jax.ShapeDty...  8.57 us
    pallas_call x1, Pallas kernels, local(): pl.pallas_call(product, out_shape=jax.ShapeDtypeStruct((PACKED, RANK), jn...  1.4 us
    ppermute x1, waiting for transfers between devices, summed(): share = share + lax.ppermute(share, 'core', [(0, 1), (1, 0)])  1.16 us
  transfers between devices with their start and end apart: 1, of which 1 were waited for; matrix products, arithmetic and copies ran while one was open for 0% of the time, Pallas kernels for 0%

profile of v6, /device:TPU:2, one launch (start us, length us, event | category | flops | bytes accessed | tf_op | source)
XLA Modules:
  0.0 54.0 jit_solution(7902471706504436425)
XLA Ops:
  0.6 1.4 %product.1 = f32[288,128]{1,0:T(8,128)S(1)} custom-call(bf16[256,1024]{1,0:T(8,128)(2,1)} %refs_2_.1), custom_call_target="tpu_custom_call" | custom-call | tf_op jit(solution)/shard_map/product/pallas_call | solution.py:272
  2.0 14.0 %all_to_all.15 = f32[16,9,2,128]{3,2,1,0:T(2,128)S(1)} all-to-all(f32[16,9,2,128]{3,2,1,0:T(2,128)S(1)} %bitcast.3), channel_id=1, replica_groups=mesh['y'=4,'x'=4,'z'=8,'core'=2] {'y','x'}, dimensions={0} | all-to-all | bytes 294912 | tf_op jit(solution)/shard_map/all_to_all | solution.py:254
  16.0 0.0 copy-start
  16.0 0.1 reduce_sum.18
  16.1 0.1 collective-permute-start
  16.2 1.2 %collective-permute-done = f32[9,2,128]{2,1,0:T(2,128)S(1)} collective-permute-done((f32[9,2,128]{2,1,0:T(2,128)S(1)}, f32[9,2,128]{2,1,0:T(2,128)S(1)}, u32[]{:S(2)}, u32[]{:S(2)}) %collective-permute-start) | collective-permute-done | bytes 9248 | tf_op jit(solution)/shard_map/ppermute | solution.py:264
  17.4 16.7 %all_to_all.16 = f32[8,9,2,128]{3,2,1,0:T(2,128)S(1)} all-to-all(f32[8,9,2,128]{3,2,1,0:T(2,128)S(1)} %broadcast_in_dim.6), channel_id=1, replica_groups=mesh['y'=4,'x'=4,'z'=8,'core'=2] {'z'}, dimensions={0} | all-to-all | bytes 147456 | tf_op jit(solution)/shard_map/all_to_all | solution.py:254
  34.2 0.0 copy-start.1
  34.2 11.3 %all_to_all.17 = f32[16,9,2,128]{3,2,1,0:T(2,128)S(1)} all-to-all(f32[16,9,2,128]{3,2,1,0:T(2,128)S(1)} %broadcast_in_dim.7), channel_id=1, replica_groups=mesh['y'=4,'x'=4,'z'=8,'core'=2] {'y','x'}, dimensions={0} | all-to-all | bytes 294912 | tf_op jit(solution)/shard_map/all_to_all | solution.py:254
  45.5 0.0 copy-done
  45.5 0.0 copy-done.1
  45.5 8.6 %algebra.1 = (f32[128,1024]{1,0:T(8,128)}, f32[128,256]{1,0:T(8,128)}) custom-call(f32[288,128]{1,0:T(8,128)S(1)} %bitcast.2, bf16[128,256]{1,0:T(8,128)(2,1)S(1)} %copy-done.1, bf16[256,1024]{1,0:T(8,128)(2,1)S(1)} %copy-done), custom_call_target="tpu_custom_call" | custom-call | tf_op jit(solution)/shard_map/algebra/pallas_call | solution.py:281
  (4 shorter events, 0.1 us)
Async XLA Ops:
  16.0 29.4 %copy-start = (bf16[256,1024]{1,0:T(8,128)(2,1)S(1)}, bf16[256,1024]{1,0:T(8,128)(2,1)}, u32[]{:S(2)}) copy-start(bf16[256,1024]{1,0:T(8,128)(2,1)} %refs_2_.1) | copy-start | bytes 1572868
  16.1 1.3 %collective-permute-start = (f32[9,2,128]{2,1,0:T(2,128)S(1)}, f32[9,2,128]{2,1,0:T(2,128)S(1)}, u32[]{:S(2)}, u32[]{:S(2)}) collective-permute-start(f32[9,2,128]{2,1,0:T(2,128)S(1)} %reduce_sum.18), channel_id=1, source_target_pairs={{0,1},{1,0},{2,3},{3,2},{4,5},{5,4},{6,7},{7,6},{8,9},{9,8},{10,11... | collective-permute-start | bytes 27656 | tf_op jit(solution)/shard_map/ppermute | solution.py:264
  34.2 11.3 %copy-start.1 = (bf16[128,256]{1,0:T(8,128)(2,1)S(1)}, bf16[128,256]{1,0:T(8,128)(2,1)}, u32[]{:S(2)}) copy-start(bf16[128,256]{1,0:T(8,128)(2,1)} %refs_1_.1) | copy-start | bytes 196612

commit v7 on v6

--- a/solution.py
+++ b/solution.py
@@ -83,14 +83,19 @@
             kept[own] = jnp.where(at[s], row, kept[own])
             here = lane == j + t
             row = jnp.where(here, 1.0, row) * inverse
-            for k in range(tall):
+            for k in range(own, tall):
                 changed = jnp.where(here, 0.0, block[k]) - columns[t][k] * row
                 block[k] = jnp.where(at[s], row, changed) if k == own else changed
             for v in range(t + 1, PANEL):
                 ratio = across[v] * inverse
-                for k in range(tall):
+                for k in range(own, tall):
                     changed = columns[v][k] - columns[t][k] * ratio
                     columns[v][k] = jnp.where(at[s], ratio, changed) if k == own else changed
+        terms = [columns[SUB + t][0] * spread(block[1][t : t + 1, :]) for t in range(SUB)]
+        while len(terms) > 1:
+            terms = [terms[k] + terms[k + 1] for k in range(0, len(terms), 2)]
+        upper = (lane >= j + SUB) & (lane < j + PANEL)
+        block[0] = jnp.where(upper, 0.0, block[0]) - terms[0]
         rows[p : p + tall] = kept
         scales += scale
         inside = (lane >= j) & (lane < j + PANEL)

time: 54.3 us -> 54.2 us (level)
  no operation moved by 1% of the time
where the time goes in v7:
time: 54.2 us; the launch traced here: 54 us
  blocking collectives  42 us (77%)
  Pallas kernels  9.91 us (18%)
  waiting for transfers between devices  1.16 us (2%)
  between operations  0.67 us (1%)
    all_to_all x3, blocking collectives, all_to_all(): return lax.all_to_all(array, axes, split_axis=0, concat_axis=0, tiled=True)  42 us
    pallas_call x1, Pallas kernels, local(): pl.pallas_call(functools.partial(algebra, cells), out_shape=(jax.ShapeDty...  8.52 us
    pallas_call x1, Pallas kernels, local(): pl.pallas_call(product, out_shape=jax.ShapeDtypeStruct((PACKED, RANK), jn...  1.4 us
    ppermute x1, waiting for transfers between devices, summed(): share = share + lax.ppermute(share, 'core', [(0, 1), (1, 0)])  1.16 us
  transfers between devices with their start and end apart: 1, of which 1 were waited for; matrix products, arithmetic and copies ran while one was open for 0% of the time, Pallas kernels for 0%

profile of v7, /device:TPU:2, one launch (start us, length us, event | category | flops | bytes accessed | tf_op | source)
XLA Modules:
  0.0 54.0 jit_solution(7985867718676053259)
XLA Ops:
  0.6 1.4 %product.1 = f32[288,128]{1,0:T(8,128)S(1)} custom-call(bf16[256,1024]{1,0:T(8,128)(2,1)} %refs_2_.1), custom_call_target="tpu_custom_call" | custom-call | tf_op jit(solution)/shard_map/product/pallas_call | solution.py:277
  2.0 14.0 %all_to_all.15 = f32[16,9,2,128]{3,2,1,0:T(2,128)S(1)} all-to-all(f32[16,9,2,128]{3,2,1,0:T(2,128)S(1)} %bitcast.3), channel_id=1, replica_groups=mesh['y'=4,'x'=4,'z'=8,'core'=2] {'y','x'}, dimensions={0} | all-to-all | bytes 294912 | tf_op jit(solution)/shard_map/all_to_all | solution.py:259
  16.0 0.0 copy-start
  16.0 0.1 reduce_sum.18
  16.1 0.1 collective-permute-start
  16.2 1.2 %collective-permute-done = f32[9,2,128]{2,1,0:T(2,128)S(1)} collective-permute-done((f32[9,2,128]{2,1,0:T(2,128)S(1)}, f32[9,2,128]{2,1,0:T(2,128)S(1)}, u32[]{:S(2)}, u32[]{:S(2)}) %collective-permute-start) | collective-permute-done | bytes 9248 | tf_op jit(solution)/shard_map/ppermute | solution.py:269
  17.4 16.7 %all_to_all.16 = f32[8,9,2,128]{3,2,1,0:T(2,128)S(1)} all-to-all(f32[8,9,2,128]{3,2,1,0:T(2,128)S(1)} %broadcast_in_dim.6), channel_id=1, replica_groups=mesh['y'=4,'x'=4,'z'=8,'core'=2] {'z'}, dimensions={0} | all-to-all | bytes 147456 | tf_op jit(solution)/shard_map/all_to_all | solution.py:259
  34.2 0.0 copy-start.1
  34.2 11.3 %all_to_all.17 = f32[16,9,2,128]{3,2,1,0:T(2,128)S(1)} all-to-all(f32[16,9,2,128]{3,2,1,0:T(2,128)S(1)} %broadcast_in_dim.7), channel_id=1, replica_groups=mesh['y'=4,'x'=4,'z'=8,'core'=2] {'y','x'}, dimensions={0} | all-to-all | bytes 294912 | tf_op jit(solution)/shard_map/all_to_all | solution.py:259
  45.5 0.0 copy-done
  45.5 0.0 copy-done.1
  45.5 8.5 %algebra.1 = (f32[128,1024]{1,0:T(8,128)}, f32[128,256]{1,0:T(8,128)}) custom-call(f32[288,128]{1,0:T(8,128)S(1)} %bitcast.2, bf16[128,256]{1,0:T(8,128)(2,1)S(1)} %copy-done.1, bf16[256,1024]{1,0:T(8,128)(2,1)S(1)} %copy-done), custom_call_target="tpu_custom_call" | custom-call | tf_op jit(solution)/shard_map/algebra/pallas_call | solution.py:286
  (4 shorter events, 0.1 us)
Async XLA Ops:
  16.0 29.4 %copy-start = (bf16[256,1024]{1,0:T(8,128)(2,1)S(1)}, bf16[256,1024]{1,0:T(8,128)(2,1)}, u32[]{:S(2)}) copy-start(bf16[256,1024]{1,0:T(8,128)(2,1)} %refs_2_.1) | copy-start | bytes 1572868
  16.1 1.3 %collective-permute-start = (f32[9,2,128]{2,1,0:T(2,128)S(1)}, f32[9,2,128]{2,1,0:T(2,128)S(1)}, u32[]{:S(2)}, u32[]{:S(2)}) collective-permute-start(f32[9,2,128]{2,1,0:T(2,128)S(1)} %reduce_sum.18), channel_id=1, source_target_pairs={{0,1},{1,0},{2,3},{3,2},{4,5},{5,4},{6,7},{7,6},{8,9},{9,8},{10,11... | collective-permute-start | bytes 27656 | tf_op jit(solution)/shard_map/ppermute | solution.py:269
  34.2 11.3 %copy-start.1 = (bf16[128,256]{1,0:T(8,128)(2,1)S(1)}, bf16[128,256]{1,0:T(8,128)(2,1)}, u32[]{:S(2)}) copy-start(bf16[128,256]{1,0:T(8,128)(2,1)} %refs_1_.1) | copy-start | bytes 196612
